TPU v7x, 32 devices: a whole 2x2x4 slice. The times are simulated.
32 devices in a mesh: fsdp: 2 (over x), ctx: 8 (over z, y), tp: 2 (over core).
Axes of the slice: x: 2, y: 2, z: 4, core: 2. Of those that a mesh axis runs over, the one named last changes fastest.
Arguments:
- tokens: bfloat16 [2, 2, 4096, 768], P(None, 'fsdp', 'ctx'), may hold values from -6 to 6
- segments: int32 [2, 2, 4096], P(None, 'fsdp', 'ctx'), may hold values from 0 to 23, never falling along the last dimension, each value on 1 to 2048 neighbouring positions
- query_weight: bfloat16 [768, 768], P(('fsdp', 'ctx'), 'tp'), may hold values from -0.21875 to 0.21875
- query_bias: float32 [768], P('tp'), may hold values from -3 to 3
- key_weight: bfloat16 [768, 64], P(('fsdp', 'ctx')), may hold values from -0.21875 to 0.21875
- key_bias: float32 [64], replicated, may hold values from -3 to 3
- value_weight: bfloat16 [768, 64], P(('fsdp', 'ctx')), may hold values from -0.21875 to 0.21875
- value_bias: float32 [64], replicated, may hold values from -3 to 3
- output_weight: bfloat16 [768, 768], P('tp', ('fsdp', 'ctx')), may hold values from -1.75 to 1.75
- output_bias: float32 [768], replicated, may hold values from -4 to 4
- upward_weight: bfloat16 [768, 3072], P(('fsdp', 'ctx'), 'tp'), may hold values from -0.21875 to 0.21875
- upward_bias: float32 [3072], P('tp'), may hold values from -3 to 3
- down_weight: bfloat16 [3072, 768], P('tp', ('fsdp', 'ctx')), may hold values from -0.109375 to 0.109375
- down_bias: float32 [768], replicated, may hold values from -4 to 4
- attend_gain: float32 [768], replicated, may hold values from 0.25 to 1.75
- attend_bias: float32 [768], replicated, may hold values from -2 to 2
- dense_gain: float32 [768], replicated, may hold values from 0.25 to 1.75
- dense_bias: float32 [768], replicated, may hold values from -2 to 2
- cotangent: bfloat16 [2, 2, 4096, 768], P(None, 'fsdp', 'ctx'), may hold values from -6 to 6
Outputs:
- result: bfloat16 [2, 2, 4096, 768], P(None, 'fsdp', 'ctx')
- tokens_grad: bfloat16 [2, 2, 4096, 768], P(None, 'fsdp', 'ctx')
- query_weight_grad: float32 [768, 768], P(('fsdp', 'ctx'), 'tp')
- query_bias_grad: float32 [768], P('tp')
- key_weight_grad: float32 [768, 64], P(('fsdp', 'ctx'))
- key_bias_grad: float32 [64], replicated
- value_weight_grad: float32 [768, 64], P(('fsdp', 'ctx'))
- value_bias_grad: float32 [64], replicated
- output_weight_grad: float32 [768, 768], P('tp', ('fsdp', 'ctx'))
- output_bias_grad: float32 [768], replicated
- upward_weight_grad: float32 [768, 3072], P(('fsdp', 'ctx'), 'tp')
- upward_bias_grad: float32 [3072], P('tp')
- down_weight_grad: float32 [3072, 768], P('tp', ('fsdp', 'ctx'))
- down_bias_grad: float32 [768], replicated
- attend_gain_grad: float32 [768], replicated
- attend_bias_grad: float32 [768], replicated
- dense_gain_grad: float32 [768], replicated
- dense_bias_grad: float32 [768], replicated
Inputs may be any that keep to these rules, and one draw needn't show every extreme that they name: `segments`: within each sequence of 4096 tokens segment numbers never fall; each of the 24 numbers is used by 1 to 2048 tokens, one by exactly 2048.
All inputs are finite; a program needn't handle non-finite values.
Results may differ from a plain program's by a relative error of at most 0.04.
Values may be sent and summed in bfloat16 or wider, within the bound.
No kernel may reach another device: no remote copies, remote signals or barrier semaphores. Data moves between devices by JAX's collectives and lax.ppermute only.
A program may use at most 128 MiB of HBM per device.

v0:
```python
import math

import jax
import jax.numpy as jnp
from jax import lax
from jax.sharding import PartitionSpec as P

ROT = 16


NEGATIVE = -1e30
EPSILON = 1e-05
key_block_limit = 512


def matmul(left, right):
    return jnp.dot(left, right, preferred_element_type=jnp.float32)


def contract_rows(left, right):
    return jnp.einsum("nd,nf->df", left, right, preferred_element_type=jnp.float32)


def contract_cols(left, right):
    return jnp.einsum("nf,df->nd", left, right, preferred_element_type=jnp.float32)


def layer_norm(values, gain, shift):
    centre = values - jnp.mean(values, axis=-1, keepdims=True)
    spread = lax.rsqrt(jnp.mean(centre * centre, axis=-1, keepdims=True) + EPSILON)
    normed = centre * spread
    return (normed * gain + shift, normed, spread)


def norm_back(grad_out, gain, normed, spread):
    scaled = grad_out * gain
    return spread * (
        scaled
        - jnp.mean(scaled, axis=-1, keepdims=True)
        - normed * jnp.mean(scaled * normed, axis=-1, keepdims=True)
    )


def rotary_tables(positions):
    freqs = jnp.exp(jnp.arange(ROT // 2, dtype=jnp.float32) * (-2.0 * math.log(10000.0) / ROT))
    angle = positions.astype(jnp.float32)[:, None] * freqs[None, :]
    return (jnp.cos(angle), jnp.sin(angle))


def rotate(values, cosine, sine):
    half = ROT // 2
    first = values[..., :half]
    second = values[..., half:ROT]
    return jnp.concatenate(
        [first * cosine - second * sine, second * cosine + first * sine, values[..., ROT:]], axis=-1
    )


def split_blocks(piece):
    width = piece.shape[0]
    block = math.gcd(width, key_block_limit)
    offsets = block * jnp.arange(width // block, dtype=jnp.int32)
    return (piece.reshape(width // block, block, piece.shape[1]), offsets, block)


def masked_scores(rows, keys, row_index, row_segment, segment_row, offset, block, scale):
    scores = scale * jnp.einsum("rd,kd->rk", rows, keys, preferred_element_type=jnp.float32)
    key_segment = lax.dynamic_slice_in_dim(segment_row, offset, block)
    key_index = offset + jnp.arange(block, dtype=jnp.int32)
    allowed = (row_segment[:, None] == key_segment[None, :]) & (
        key_index[None, :] <= row_index[:, None]
    )
    return (scores, allowed)


def to_rows(values, local_heads, head):
    count = values.shape[0]
    return jnp.transpose(values.reshape(count, local_heads, head), (1, 0, 2)).reshape(
        local_heads * count, head
    )


def from_rows(rows, local_heads, head):
    count = rows.shape[0] // local_heads
    return jnp.transpose(rows.reshape(local_heads, count, head), (1, 0, 2))


def finish(big, small):
    head = small[1].shape[0] // 2
    weight_terms = (big[0], big[1][:, :head], big[1][:, head:], big[2], big[3], big[4])
    reduced_big = (
        lax.psum_scatter(weight_terms[0], ("fsdp", "ctx"), scatter_dimension=0, tiled=True),
        lax.psum_scatter(weight_terms[1], ("fsdp", "ctx"), scatter_dimension=0, tiled=True),
        lax.psum_scatter(weight_terms[2], ("fsdp", "ctx"), scatter_dimension=0, tiled=True),
        lax.psum_scatter(weight_terms[3], ("fsdp", "ctx"), scatter_dimension=1, tiled=True),
        lax.psum_scatter(weight_terms[4], ("fsdp", "ctx"), scatter_dimension=0, tiled=True),
        lax.psum_scatter(weight_terms[5], ("fsdp", "ctx"), scatter_dimension=1, tiled=True),
    )
    bias_terms = (
        small[0],
        small[1][:head],
        small[1][head:],
        small[2],
        small[3],
        small[4],
        small[5],
        small[6],
        small[7],
    )
    reduced_small = lax.psum(
        (
            bias_terms[0],
            bias_terms[1],
            bias_terms[2],
            bias_terms[3],
            bias_terms[4],
            bias_terms[5],
            bias_terms[6],
            bias_terms[7],
            bias_terms[8],
        ),
        ("fsdp", "ctx"),
    )
    return (reduced_big, reduced_small)


def shards(
    tokens,
    segments,
    query_weight,
    query_bias,
    key_weight,
    key_bias,
    value_weight,
    value_bias,
    output_weight,
    output_bias,
    upward_weight,
    upward_bias,
    down_weight,
    down_bias,
    attend_gain,
    attend_bias,
    dense_gain,
    dense_bias,
    cotangent,
):
    micro = tokens.shape[0]
    length = tokens.shape[2]
    width = tokens.shape[3]
    head = key_weight.shape[1]
    query_width = query_bias.shape[0]
    local_heads = query_width // head
    hidden_width = upward_bias.shape[0]
    scale = head ** (-0.5)
    segment_all = lax.all_gather(segments, "ctx", axis=2, tiled=True)
    local_index = lax.axis_index("ctx") * length + jnp.arange(length, dtype=jnp.int32)
    row_index = jnp.tile(local_index, local_heads)
    bias_pair = jnp.concatenate([key_bias, value_bias])
    big = (
        jnp.zeros((width, query_width), jnp.float32),
        jnp.zeros((width, 2 * head), jnp.float32),
        jnp.zeros((query_width, width), jnp.float32),
        jnp.zeros((width, hidden_width), jnp.float32),
        jnp.zeros((hidden_width, width), jnp.float32),
    )
    small = (
        jnp.zeros((query_width,), jnp.float32),
        jnp.zeros((2 * head,), jnp.float32),
        jnp.zeros((width,), jnp.float32),
        jnp.zeros((hidden_width,), jnp.float32),
        jnp.zeros((width,), jnp.float32),
        jnp.zeros((width,), jnp.float32),
        jnp.zeros((width,), jnp.float32),
        jnp.zeros((width,), jnp.float32),
    )
    big, small = (big, small)
    summed = None
    results = []
    input_grads = []
    for micro_index in range(micro):
        gathered = (
            lax.all_gather(query_weight, ("fsdp", "ctx"), axis=0, tiled=True),
            lax.all_gather(key_weight, ("fsdp", "ctx"), axis=0, tiled=True),
            lax.all_gather(value_weight, ("fsdp", "ctx"), axis=0, tiled=True),
            lax.all_gather(output_weight, ("fsdp", "ctx"), axis=1, tiled=True),
            lax.all_gather(upward_weight, ("fsdp", "ctx"), axis=0, tiled=True),
            lax.all_gather(down_weight, ("fsdp", "ctx"), axis=1, tiled=True),
        )
        w_query, w_key, w_value, w_output, w_upward, w_down = gathered
        w_pair = jnp.concatenate([w_key, w_value], axis=1)
        inputs = tokens[micro_index, 0].astype(jnp.float32)
        seg_local = segments[micro_index, 0]
        segment_row = segment_all[micro_index, 0]
        positions = local_index - jnp.sum(
            (segment_row[None, :] < seg_local[:, None]).astype(jnp.int32), axis=1
        )
        cosine, sine = rotary_tables(positions)
        row_segment = jnp.tile(seg_local, local_heads)
        attend_norm, attend_normed, attend_spread = layer_norm(inputs, attend_gain, attend_bias)
        dense_norm, dense_normed, dense_spread = layer_norm(inputs, dense_gain, dense_bias)
        attend_in = attend_norm.astype(jnp.bfloat16)
        dense_in = dense_norm.astype(jnp.bfloat16)
        query_lin = (matmul(attend_in, w_query) + query_bias).reshape(length, local_heads, head)
        query_rot = rotate(query_lin, cosine[:, None, :], sine[:, None, :]).astype(jnp.bfloat16)
        rows = jnp.transpose(query_rot, (1, 0, 2)).reshape(local_heads * length, head)
        pair_lin = matmul(attend_in, w_pair) + bias_pair
        pair_send = jnp.concatenate(
            [rotate(pair_lin[:, :head], cosine, sine), pair_lin[:, head:]], axis=1
        ).astype(jnp.bfloat16)
        row_count = local_heads * length
        start_state = (
            jnp.full((row_count,), NEGATIVE, jnp.float32),
            jnp.zeros((row_count,), jnp.float32),
            jnp.zeros((row_count, head), jnp.float32),
        )
        state = start_state
        blocks, offsets, block = split_blocks(lax.all_gather(pair_send, "ctx", axis=0, tiled=True))

        def forward_inner(carry, item):
            best, total, accum = carry
            key_value, offset = item
            scores, allowed = masked_scores(
                rows, key_value[:, :head], row_index, row_segment, segment_row, offset, block, scale
            )
            fresh = jnp.maximum(best, jnp.max(jnp.where(allowed, scores, NEGATIVE), axis=1))
            weights = jnp.where(allowed, jnp.exp(scores - fresh[:, None]), 0.0)
            factor = jnp.exp(best - fresh)
            total = total * factor + jnp.sum(weights, axis=1)
            accum = accum * factor[:, None] + matmul(
                weights.astype(jnp.bfloat16), key_value[:, head:]
            )
            return ((fresh, total, accum), None)

        state, unused = lax.scan(forward_inner, state, (blocks, offsets))
        best, total, accum = state
        out_rows = accum / total[:, None]
        logsum = best + jnp.log(total)
        attended_low = from_rows(out_rows.astype(jnp.bfloat16), local_heads, head).reshape(
            length, query_width
        )
        hidden_pre = matmul(dense_in, w_upward) + upward_bias
        hidden = jax.nn.gelu(hidden_pre, approximate=False).astype(jnp.bfloat16)
        branches = matmul(attended_low, w_output) + matmul(hidden, w_down)
        mixed = lax.psum(branches.astype(jnp.bfloat16), "tp").astype(jnp.float32)
        results.append((inputs + mixed + output_bias + down_bias).astype(jnp.bfloat16))
        grad_low = cotangent[micro_index, 0]
        grad_full = grad_low.astype(jnp.float32)
        grad_out_weight = contract_rows(attended_low, grad_low)
        grad_down_weight = contract_rows(hidden, grad_low)
        grad_out_bias = jnp.sum(grad_full, axis=0)
        attended_grad = contract_cols(grad_low, w_output).astype(jnp.bfloat16)
        grad_rows = to_rows(attended_grad, local_heads, head)
        delta = jnp.sum(grad_rows.astype(jnp.float32) * out_rows, axis=1)
        hidden_grad = contract_cols(grad_low, w_down)
        normal_cdf = 0.5 * (1.0 + jax.scipy.special.erf(hidden_pre * (1.0 / math.sqrt(2.0))))
        normal_pdf = jnp.exp(-0.5 * hidden_pre * hidden_pre) * (1.0 / math.sqrt(2.0 * math.pi))
        pre_grad = (hidden_grad * (normal_cdf + hidden_pre * normal_pdf)).astype(jnp.bfloat16)
        grad_up_weight = contract_rows(dense_in, pre_grad)
        grad_up_bias = jnp.sum(pre_grad.astype(jnp.float32), axis=0)
        dense_part = contract_cols(pre_grad, w_upward)
        piece = lax.all_gather(pair_send, "ctx", axis=0, tiled=True)
        query_acc = jnp.zeros((row_count, head), jnp.float32)
        backward_blocks, backward_offsets, backward_block = split_blocks(piece)

        def backward_inner(carry, item):
            key_value, offset = item
            keys = key_value[:, :head]
            scores, allowed = masked_scores(
                rows, keys, row_index, row_segment, segment_row, offset, backward_block, scale
            )
            probs = jnp.where(allowed, jnp.exp(scores - logsum[:, None]), 0.0)
            value_grad = jnp.einsum(
                "rk,rd->kd",
                probs.astype(jnp.bfloat16),
                grad_rows,
                preferred_element_type=jnp.float32,
            )
            prob_grad = jnp.einsum(
                "rd,kd->rk", grad_rows, key_value[:, head:], preferred_element_type=jnp.float32
            )
            score_grad = (probs * (prob_grad - delta[:, None])).astype(jnp.bfloat16)
            carry = carry + scale * matmul(score_grad, keys)
            key_grad = scale * jnp.einsum(
                "rk,rd->kd", score_grad, rows, preferred_element_type=jnp.float32
            )
            return (carry, jnp.concatenate([key_grad, value_grad], axis=1))

        query_acc, pieces = lax.scan(backward_inner, query_acc, (backward_blocks, backward_offsets))
        buffer = pieces.reshape(piece.shape[0], 2 * head)
        pair_partial = lax.psum_scatter(
            buffer.astype(jnp.bfloat16), "ctx", scatter_dimension=0, tiled=True
        )
        query_back = rotate(
            from_rows(query_acc, local_heads, head), cosine[:, None, :], -sine[:, None, :]
        )
        query_grad = query_back.astype(jnp.bfloat16).reshape(length, query_width)
        grad_query_weight = contract_rows(attend_in, query_grad)
        grad_query_bias = jnp.sum(query_grad.astype(jnp.float32), axis=0)
        attend_part = contract_cols(query_grad, w_query)
        attend_sum, dense_grad, pair_grad = (
            lax.psum(attend_part.astype(jnp.bfloat16), "tp").astype(jnp.float32),
            lax.psum(dense_part.astype(jnp.bfloat16), "tp").astype(jnp.float32),
            lax.psum(pair_partial, "tp").astype(jnp.float32),
        )
        pair_low = jnp.concatenate(
            [rotate(pair_grad[:, :head], cosine, -sine), pair_grad[:, head:]], axis=1
        ).astype(jnp.bfloat16)
        attend_grad = attend_sum + contract_cols(pair_low, w_pair)
        input_grads.append(
            (
                grad_full
                + norm_back(attend_grad, attend_gain, attend_normed, attend_spread)
                + norm_back(dense_grad, dense_gain, dense_normed, dense_spread)
            ).astype(jnp.bfloat16)
        )
        grad_pair_weight = contract_rows(attend_in, pair_low)
        grad_pair_bias = jnp.sum(pair_low.astype(jnp.float32), axis=0)
        fresh_big = (
            grad_query_weight,
            grad_pair_weight,
            grad_out_weight,
            grad_up_weight,
            grad_down_weight,
        )
        fresh_small = (
            grad_query_bias,
            grad_pair_bias,
            grad_out_bias,
            grad_up_bias,
            jnp.sum(attend_grad * attend_normed, axis=0),
            jnp.sum(attend_grad, axis=0),
            jnp.sum(dense_grad * dense_normed, axis=0),
            jnp.sum(dense_grad, axis=0),
        )
        big = jax.tree.map(jnp.add, big, fresh_big)
        small = jax.tree.map(jnp.add, small, fresh_small)
    summed = finish(big, small)
    weight_grads, bias_grads = summed
    result = jnp.stack(results)[:, None]
    tokens_grad = jnp.stack(input_grads)[:, None]
    return (
        result,
        tokens_grad,
        weight_grads[0],
        bias_grads[0],
        weight_grads[1],
        bias_grads[1],
        weight_grads[2],
        bias_grads[2],
        weight_grads[3],
        bias_grads[3],
        weight_grads[4],
        bias_grads[4],
        weight_grads[5],
        bias_grads[3],
        bias_grads[5],
        bias_grads[6],
        bias_grads[7],
        bias_grads[8],
    )


def solution(mesh):
    return jax.shard_map(
        shards,
        mesh=mesh,
        in_specs=(
            P(None, "fsdp", "ctx", None),
            P(None, "fsdp", "ctx"),
            P(("fsdp", "ctx"), "tp"),
            P("tp"),
            P(("fsdp", "ctx"), None),
            P(),
            P(("fsdp", "ctx"), None),
            P(),
            P("tp", ("fsdp", "ctx")),
            P(),
            P(("fsdp", "ctx"), "tp"),
            P("tp"),
            P("tp", ("fsdp", "ctx")),
            P(),
            P(),
            P(),
            P(),
            P(),
            P(None, "fsdp", "ctx", None),
        ),
        out_specs=(
            P(None, "fsdp", "ctx", None),
            P(None, "fsdp", "ctx", None),
            P(("fsdp", "ctx"), "tp"),
            P("tp"),
            P(("fsdp", "ctx"), None),
            P(),
            P(("fsdp", "ctx"), None),
            P(),
            P("tp", ("fsdp", "ctx")),
            P(),
            P(("fsdp", "ctx"), "tp"),
            P("tp"),
            P("tp", ("fsdp", "ctx")),
            P(),
            P(),
            P(),
            P(),
            P(),
        ),
        check_vma=False,
    )
```

profile of v0, /device:TPU:0, one launch (start us, length us, event | category | flops | bytes accessed | tf_op | source)
XLA Modules:
  0.0 1655.1 jit_solution(1305914401162070729)
XLA Ops:
  7.3 28.1 %all_gather.35 = s32[2,1,4096]{2,1,0:T(1,128)S(1)} all-gather(s32[2,1,512]{2,1,0:T(1,128)} %param.28), channel_id=1, replica_groups=mesh['fsdp'=2,'ctx'=8,'tp'=2] {'ctx'}, dimensions={2}, use_global_device_ids=true | all-gather | bytes 36864 | tf_op jit(solution)/shard_map/all_gather | solution.py:156
  37.8 40.2 %all_gather.36 = bf16[768,64]{1,0:T(8,128)(2,1)S(1)} all-gather(bf16[48,64]{1,0:T(8,128)(2,1)} %param.31), channel_id=1, replica_groups=mesh['fsdp'=2,'ctx'=8,'tp'=2] {'fsdp','ctx'}, dimensions={0}, use_global_device_ids=true | all-gather | bytes 104448 | tf_op jit(solution)/shard_map/all_gather | solution.py:184
  78.0 36.8 %all_gather.37 = bf16[768,64]{1,0:T(8,128)(2,1)S(1)} all-gather(bf16[48,64]{1,0:T(8,128)(2,1)} %param.33), channel_id=1, replica_groups=mesh['fsdp'=2,'ctx'=8,'tp'=2] {'fsdp','ctx'}, dimensions={0}, use_global_device_ids=true | all-gather | bytes 104448 | tf_op jit(solution)/shard_map/all_gather | solution.py:185
  124.3 42.2 %all_gather.39 = bf16[768,384]{1,0:T(8,128)(2,1)S(1)} all-gather(bf16[48,384]{1,0:T(8,128)(2,1)S(1)} %copy-done.51), channel_id=1, replica_groups=mesh['fsdp'=2,'ctx'=8,'tp'=2] {'fsdp','ctx'}, dimensions={0}, use_global_device_ids=true | all-gather | bytes 626688 | tf_op jit(solution)/shard_map/all_gather | solution.py:183
  171.1 41.2 %all_gather.40 = bf16[384,768]{0,1:T(8,128)(2,1)S(1)} all-gather(bf16[384,48]{0,1:T(8,128)(2,1)S(1)} %copy-done.52), channel_id=1, replica_groups=mesh['fsdp'=2,'ctx'=8,'tp'=2] {'fsdp','ctx'}, dimensions={1}, use_global_device_ids=true | all-gather | bytes 626688 | tf_op jit(solution)/shard_map/all_gather | solution.py:186
  222.7 129.7 %while.56 = (s32[]{:T(128)}, f32[3072]{0:T(1024)S(1)}, f32[3072]{0:T(1024)S(1)}, f32[3072,64]{0,1:T(8,128)S(1)}, s32[8]{0:T(128)}, /*index=5*/s32[4096]{0:T(1024...) while((s32[]{:T(128)}, f32[3072]{0:T(1024)S(1)}, ...), condition=%wide.region_6.7_spmd.clone, body=%wide.region_3.6_spmd.clone.sunk | while | flops 434716160 | bytes 46897372 | solution.py:235
  276.1 4.7 fusion.350
  355.5 128.8 %while.57 = (s32[]{:T(128)}, f32[3072]{0:T(1024)S(1)}, f32[3072]{0:T(1024)S(1)}, f32[3072,64]{0,1:T(8,128)S(1)}, s32[8]{0:T(128)}, /*index=5*/s32[4096]{0:T(1024...) while((s32[]{:T(128)}, f32[3072]{0:T(1024)S(1)}, ...), condition=%wide.region_14.15_spmd.clone, body=%wide.region_11.14_spmd.clone.sunk | while | flops 434716160 | bytes 46897372 | solution.py:235
  485.6 125.4 %while.58 = (s32[]{:T(128)}, f32[3072,64]{0,1:T(8,128)}, bf16[8,512,128]{1,2,0:T(8,128)(2,1)}, s32[8]{0:T(128)}, s32[4096]{0:T(1024)S(1)}, /*index=5*/bf16[8,512...) while((s32[]{:T(128)}, f32[3072,64]{0,1:T(8,128)}, ...), condition=%wide.region_18.19_spmd.clone, body=%wide.region_17.18_spmd.clone.sunk | while | flops 1023279616 | bytes 34216684 | solution.py:289
  616.7 125.2 %while.59 = (s32[]{:T(128)}, f32[3072,64]{0,1:T(8,128)}, bf16[8,512,128]{1,2,0:T(8,128)(2,1)}, s32[8]{0:T(128)}, s32[4096]{0:T(1024)S(1)}, /*index=5*/bf16[8,512...) while((s32[]{:T(128)}, f32[3072,64]{0,1:T(8,128)}, ...), condition=%wide.region_29.30_spmd.clone, body=%wide.region_28.29_spmd.clone.sunk | while | flops 1023279616 | bytes 34216684 | solution.py:289
  756.5 11.3 fusion.62
  773.3 7.9 fusion.65
  795.7 22.2 %reduce-scatter.15.cloned.1.call-done = bf16[512,128]{0,1:T(8,128)(2,1)} async-done(((bf16[4096,128]{0,1:T(8,128)(2,1)}), bf16[512,128]{0,1:T(8,128)(2,1)}) %reduce-scatter.15.cloned.1.call-update) | async-done | bytes 131088 | tf_op jit(solution)/shard_map/reduce_scatter | solution.py:291
  826.0 24.5 %all-reduce.4.cloned.1.call-done = (bf16[512,768]{1,0:T(8,128)(2,1)}, bf16[512,768]{1,0:T(8,128)(2,1)}, bf16[512,768]{1,0:T(8,128)(2,1)}, bf16[512,768]{1,0:T(8,...) async-done(((bf16[512,768]{1,0:T(8,128)(2,1)}, bf16[512,768]{1,0:T(8,128)(2,1)}, ...) | async-done | bytes 4980752 | tf_op jit(solution)/shard_map/psum | solution.py:245
  859.2 5.2 fusion.240
  865.3 6.6 convolution_add_fusion.3
  884.2 5.5 fusion.158
  892.3 77.6 %all-reduce = (f32[384]{0:T(512)}, f32[64]{0:T(128)}, f32[64]{0:T(128)}, f32[768]{0:T(1024)S(1)}, f32[1536]{0:T(1024)}, /*index=5*/f32[768]{0:T(1024)}, f32[768]{0:T(1024)}, f32[768]{0:T(1024)}, f32[768]{0:T(1024)}) all-reduce(f32[384]{0:T(512)S(1)} %copy-done.73, ...), channel_id=1, replica_groups=mesh['fsdp'=2,'ctx'=8,'tp'=2] {'fsdp','ctx'}, use_global_device_ids=true, to_apply=%region_41.42 | all-reduce | flops 5888 | bytes 47104 | tf_op jit(solution)/shard_map/psum | solution.py:110
  975.8 5.7 reduce-scatter.17.cloned.1.call-done
  981.5 128.8 %reduce-scatter.19.cloned.1.call-done = f32[384,48]{0,1:T(8,128)} async-done(((f32[384,768]{0,1:T(8,128)}), f32[384,48]{0,1:T(8,128)}) %reduce-scatter.19.cloned.1.call-update) | async-done | bytes 73744 | tf_op jit(solution)/shard_map/reduce_scatter | solution.py:95
  1110.3 126.2 %reduce-scatter.25.cloned.1.call-done = f32[48,64]{1,0:T(8,128)} async-done(((f32[768,64]{1,0:T(8,128)}), f32[48,64]{1,0:T(8,128)}) %reduce-scatter.25.cloned.1.call-update) | async-done | bytes 12304
  1236.5 125.7 %reduce-scatter.27.cloned.1.call-done = f32[48,64]{1,0:T(8,128)} async-done(((f32[768,64]{1,0:T(8,128)}), f32[48,64]{1,0:T(8,128)}) %reduce-scatter.27.cloned.1.call-update) | async-done | bytes 12304
  1362.2 143.4 %reduce-scatter.21.cloned.1.call-done = f32[48,1536]{1,0:T(8,128)} async-done(((f32[768,1536]{1,0:T(8,128)}), f32[48,1536]{1,0:T(8,128)}) %reduce-scatter.21.cloned.1.call-update) | async-done | bytes 294928 | tf_op jit(solution)/shard_map/reduce_scatter | solution.py:96
  1505.6 142.2 %reduce-scatter.23.cloned.1.call-done = f32[1536,48]{0,1:T(8,128)} async-done(((f32[1536,768]{0,1:T(8,128)}), f32[1536,48]{0,1:T(8,128)}) %reduce-scatter.23.cloned.1.call-update) | async-done | bytes 294928 | tf_op jit(solution)/shard_map/reduce_scatter | solution.py:97
  (852 shorter events, 548.7 us)
Async XLA Ops:
  7.2 109.9 %copy-start.5 = (bf16[2,1,512,768]{3,2,1,0:T(8,128)(2,1)S(1)}, bf16[2,1,512,768]{3,2,1,0:T(8,128)(2,1)}, u32[]{:S(2)}) copy-start(bf16[2,1,512,768]{3,2,1,0:T(8,128)(2,1)} %param.27) | copy-start | bytes 4718596
  7.2 109.7 %copy-start.91 = (f32[64]{0:T(128)S(1)}, f32[64]{0:T(128)}, u32[]{:S(2)}) copy-start(f32[64]{0:T(128)} %param.32) | copy-start | bytes 772
  7.2 109.7 %copy-start.90 = (f32[64]{0:T(128)S(1)}, f32[64]{0:T(128)}, u32[]{:S(2)}) copy-start(f32[64]{0:T(128)} %param.34) | copy-start | bytes 772
  7.2 109.8 %copy-start.49 = (f32[768]{0:T(1024)S(1)}, f32[768]{0:T(1024)}, u32[]{:S(2)}) copy-start(f32[768]{0:T(1024)} %param.41) | copy-start | bytes 9220
  7.2 109.8 %copy-start.74 = (f32[768]{0:T(1024)S(1)}, f32[768]{0:T(1024)}, u32[]{:S(2)}) copy-start(f32[768]{0:T(1024)} %param.42) | copy-start | bytes 9220
  7.2 213.2 %all-gather.5.cloned.1.call-start = ((), (), s32[]{:S(2)}) async-start(), calls=%async_computation.8 | async-start | bytes 1179648 | tf_op jit(solution)/shard_map/all_gather | solution.py:218
  37.8 131.4 %copy-start.47 = (f32[512]{0:T(512)}, f32[512]{0:T(512)S(1)}, u32[]{:S(2)}) copy-start(f32[512]{0:T(512)S(1)} %broadcast_multiply_fusion.8) | copy-start | bytes 6148
  121.4 92.7 %copy-start.37 = (f32[512,8]{0,1:T(8,128)}, f32[512,8]{0,1:T(8,128)S(1)}, u32[]{:S(2)}) copy-start(f32[512,8]{0,1:T(8,128)S(1)} %get-tuple-element.1118) | copy-start | bytes 49156
  121.4 96.3 %copy-start.35 = (f32[512,8]{0,1:T(8,128)}, f32[512,8]{0,1:T(8,128)S(1)}, u32[]{:S(2)}) copy-start(f32[512,8]{0,1:T(8,128)S(1)} %get-tuple-element.1110) | copy-start | bytes 49156
  122.1 231.2 %all-gather.11.cloned.1.call-start = ((), (), s32[]{:S(2)}) async-start(), calls=%async_computation.11 | async-start | bytes 1179648 | tf_op jit(solution)/shard_map/all_gather | solution.py:218
  122.9 633.5 %all-gather.7.cloned.1.call-start = ((), (), s32[]{:S(2)}) async-start(), calls=%async_computation.9 | async-start | bytes 2506752 | tf_op jit(solution)/shard_map/all_gather | solution.py:187
  123.6 644.1 %all-gather.9.cloned.1.call-start = ((), (), s32[]{:S(2)}) async-start(), calls=%async_computation.10 | async-start | bytes 2506752 | tf_op jit(solution)/shard_map/all_gather | solution.py:188
  124.2 671.5 %reduce-scatter.13.cloned.1.call-start = ((), (), s32[]{:S(2)}) async-start(), calls=%async_computation.12 | async-start | bytes 1179648 | tf_op jit(solution)/shard_map/reduce_scatter | solution.py:291
  615.6 202.2 %reduce-scatter.15.cloned.1.call-start = ((), (), s32[]{:S(2)}) async-start(), calls=%async_computation.13 | async-start | bytes 1179648 | tf_op jit(solution)/shard_map/reduce_scatter | solution.py:291
  616.7 126.9 %copy-start.38 = (f32[512,8]{0,1:T(8,128)S(1)}, f32[512,8]{0,1:T(8,128)}, u32[]{:S(2)}) copy-start(f32[512,8]{0,1:T(8,128)} %copy-done.37) | copy-start | bytes 49156
  616.7 126.9 %copy-start.45 = (f32[512,8]{0,1:T(8,128)S(1)}, f32[512,8]{0,1:T(8,128)}, u32[]{:S(2)}) copy-start(f32[512,8]{0,1:T(8,128)} %get-tuple-element.1119) | copy-start | bytes 49156
  756.3 94.2 %all-reduce.4.cloned.1.call-start = ((), (), s32[]{:S(2)}) async-start(), calls=%async_computation.20 | async-start | bytes 9961472 | tf_op jit(solution)/shard_map/psum | solution.py:245
  817.9 163.6 %reduce-scatter.17.cloned.1.call-start = ((), (), s32[]{:S(2)}) async-start(), calls=%async_computation.14 | async-start | bytes 1253376 | tf_op jit(solution)/shard_map/reduce_scatter | solution.py:92
  822.5 287.8 %reduce-scatter.19.cloned.1.call-start = ((), (), s32[]{:S(2)}) async-start(), calls=%async_computation.15 | async-start | bytes 1253376 | tf_op jit(solution)/shard_map/reduce_scatter | solution.py:95
  826.0 410.5 %reduce-scatter.25.cloned.1.call-start = ((), (), s32[]{:S(2)}) async-start(), calls=%async_computation.18 | async-start | bytes 417792
  859.1 503.1 %reduce-scatter.27.cloned.1.call-start = ((), (), s32[]{:S(2)}) async-start(), calls=%async_computation.19 | async-start | bytes 417792
  865.3 640.3 %reduce-scatter.21.cloned.1.call-start = ((), (), s32[]{:S(2)}) async-start(), calls=%async_computation.16 | async-start | bytes 5013504 | tf_op jit(solution)/shard_map/reduce_scatter | solution.py:96
  872.0 775.8 %reduce-scatter.23.cloned.1.call-start = ((), (), s32[]{:S(2)}) async-start(), calls=%async_computation.17 | async-start | bytes 5013504 | tf_op jit(solution)/shard_map/reduce_scatter | solution.py:97
  969.9 677.9 %copy-start.79 = (f32[768]{0:T(1024)}, f32[768]{0:T(1024)S(1)}, u32[]{:S(2)}) copy-start(f32[768]{0:T(1024)S(1)} %get-tuple-element.1618) | copy-start | bytes 9220
  (111 other events, 1651.9 us)
Sparse Core Ops, SparseCore 0:
  122.2 42.0 all-gather.4
  166.9 40.5 all-gather.10
  210.2 60.8 all-gather.6
  273.6 61.1 all-gather.8
  615.7 61.3 reduce-scatter.12
  756.5 61.3 reduce-scatter.14
  821.2 29.3 all-reduce.3
  856.6 124.8 reduce-scatter.16
  987.5 122.7 reduce-scatter.18
  1116.1 120.3 reduce-scatter.24
  1241.7 120.4 reduce-scatter.26
  1368.6 136.9 reduce-scatter.20
  1511.3 136.4 reduce-scatter.22
where the time goes:
time: 1670 us; the launch traced here: 1660 us
  waiting for transfers between devices  720 us (43%)
  matrix products  347 us (21%)
  blocking collectives  266 us (16%)
  other arithmetic  127 us (8%)
  local copies, waits for them, and re-layouts  113 us (7%)
  loops' own time  65 us (4%)
    unnamed x15, waiting for transfers between devices  253 us
    reduce_scatter x1, waiting for transfers between devices, finish(): lax.psum_scatter(weight_terms[4], ('fsdp', 'ctx'), scatter_dimension=0, t...  143 us
    reduce_scatter x1, waiting for transfers between devices, finish(): lax.psum_scatter(weight_terms[5], ('fsdp', 'ctx'), scatter_dimension=1, t...  142 us
    reduce_scatter x1, waiting for transfers between devices, finish(): lax.psum_scatter(weight_terms[3], ('fsdp', 'ctx'), scatter_dimension=1, t...  129 us
    dot_general x32, matrix products, masked_scores(): jnp.einsum('rd,kd->rk', rows, keys, preferred_element_type=jnp.float32)  124 us
    dot_general x42, matrix products, matmul(): return jnp.dot(left, right, preferred_element_type=jnp.float32)  103 us
    psum x1, blocking collectives, finish(): lax.psum((bias_terms[0], bias_terms[1], bias_terms[2], bias_terms[3], bia...  77.6 us
    reduce_sum x16, other arithmetic, forward_inner(): total = total * factor + jnp.sum(weights, axis=1)  70.2 us
  transfers between devices with their start and end apart: 13, of which 8 were waited for; matrix products, arithmetic and copies ran while one was open for 34% of the time, Pallas kernels for 0%

commit v1 on v0

v1 whole, which is shorter than its diff:
```python
import functools
import math

import jax
import jax.numpy as jnp
from jax import lax
from jax.experimental import pallas as pl
from jax.experimental.pallas import tpu as pltpu
from jax.sharding import PartitionSpec as P

ROT = 16
NEGATIVE = -1e30
EPSILON = 1e-05
LOG2E = math.log2(math.e)
LANES = 128
query_block = 256
key_block = 256
SHARDED = ("fsdp", "ctx")


def dot(left, right, left_dim, right_dim):
    return lax.dot_general(
        left,
        right,
        (((left_dim,), (right_dim,)), ((), ())),
        preferred_element_type=jnp.float32,
    )


def axis_bits(name):
    return [1 << b for b in reversed(range(lax.axis_size(name).bit_length() - 1))]


def all_bits():
    return [("fsdp", d) for d in axis_bits("fsdp")] + [("ctx", d) for d in axis_bits("ctx")]


def partner(values, stage):
    name, distance = stage
    pairs = [(i, i ^ distance) for i in range(lax.axis_size(name))]
    return lax.ppermute(values, name, pairs)


def own_bit(stage):
    name, distance = stage
    return (lax.axis_index(name) // distance) % 2 == 1


def gather_shards(piece, order):
    rank = {stage: i for i, stage in enumerate(all_bits())}
    held = piece[None]
    done = []
    for stage in order:
        low = 1 << sum(rank[other] > rank[stage] for other in done)
        split = held.reshape((held.shape[0] // low, 1, low) + piece.shape)
        other = partner(held, stage).reshape(split.shape)
        upper = own_bit(stage)
        held = jnp.concatenate(
            [jnp.where(upper, other, split), jnp.where(upper, split, other)], axis=1
        ).reshape((2 * held.shape[0],) + piece.shape)
        done.append(stage)
    return held


def scatter_sum(terms, order):
    rank = {stage: i for i, stage in enumerate(all_bits())}
    left = list(rank)
    held = terms
    for stage in order:
        left.remove(stage)
        low = 1 << sum(rank[other] > rank[stage] for other in left)
        split = held.reshape((held.shape[0] // (2 * low), 2, low) + terms.shape[1:])
        upper = own_bit(stage)
        shape = (held.shape[0] // 2,) + terms.shape[1:]
        send = jnp.where(upper, split[:, 0], split[:, 1]).reshape(shape)
        keep = jnp.where(upper, split[:, 1], split[:, 0]).reshape(shape)
        total = keep.astype(jnp.float32) + partner(send, stage).astype(jnp.float32)
        held = total.astype(jnp.bfloat16) if left else total
    return held[0]


def total_sum(values, stages):
    for stage in stages:
        values = values + partner(values, stage)
    return values


def norm_parts(values):
    centre = values - jnp.mean(values, axis=-1, keepdims=True)
    spread = lax.rsqrt(jnp.mean(centre * centre, axis=-1, keepdims=True) + EPSILON)
    return centre * spread, spread


def rotate(values, cosine, sine):
    half = ROT // 2
    first = values[..., :half, :]
    second = values[..., half:ROT, :]
    return jnp.concatenate(
        [first * cosine - second * sine, second * cosine + first * sine, values[..., ROT:, :]],
        axis=-2,
    )


def block_plan(start, before, micro, length):
    first = start[:, ::query_block]
    last = start[:, query_block - 1 :: query_block]
    begin = before + query_block * jnp.arange(length // query_block, dtype=jnp.int32)[None]
    lo = first // key_block
    hi = jnp.broadcast_to((begin + query_block - 1) // key_block + 1, lo.shape)
    a = jnp.clip((last + key_block - 1) // key_block, lo, hi)
    b = jnp.clip((begin + 1) // key_block, a, hi)
    return jnp.stack([lo, hi, a, b], axis=-1).reshape(-1)


def allowed_pairs(block, start, begin):
    shape = (key_block, query_block)
    key_index = block * key_block + lax.broadcasted_iota(jnp.int32, shape, 0)
    query_index = begin + lax.broadcasted_iota(jnp.int32, shape, 1)
    return (key_index >= start) & (key_index <= query_index)


def over_blocks(plan, at, body):
    lo, hi, a, b = plan[at], plan[at + 1], plan[at + 2], plan[at + 3]

    def step(block, carry):
        inside = (block >= a) & (block < b)

        @pl.when(inside)
        def _():
            body(block, False)

        @pl.when(jnp.logical_not(inside))
        def _():
            body(block, True)

        return carry

    lax.fori_loop(lo, hi, step, 0)


def forward_kernel(before, heads, head, plan, query, pair, start, out, out_low, logsum, best, total):
    at = pl.program_id(0) * pl.num_programs(1) + pl.program_id(1)
    begin = before + pl.program_id(1) * query_block
    factor = head**-0.5 * LOG2E
    best[...] = jnp.full(best.shape, NEGATIVE, jnp.float32)
    total[...] = jnp.zeros(total.shape, jnp.float32)
    out[...] = jnp.zeros(out.shape, jnp.float32)

    def body(block, masked):
        keys = pl.ds(pl.multiple_of(block * key_block, key_block), key_block)
        key = pair[0, :head, keys].T
        value = pair[0, head:, keys]
        if masked:
            allowed = allowed_pairs(block, start[...], begin)
        for h in range(heads):
            rows = pl.ds(h * head, head)
            scores = dot(key, query[rows, :], 1, 0) * factor
            if masked:
                scores = jnp.where(allowed, scores, NEGATIVE)
            old = best[pl.ds(h, 1), :]
            fresh = jnp.maximum(old, jnp.max(scores, axis=0, keepdims=True))
            weights = jnp.exp2(scores - fresh)
            shrink = jnp.exp2(old - fresh)
            best[pl.ds(h, 1), :] = fresh
            total[pl.ds(h, 1), :] = total[pl.ds(h, 1), :] * shrink + jnp.sum(
                weights, axis=0, keepdims=True
            )
            out[rows, :] = out[rows, :] * shrink + dot(value, weights.astype(jnp.bfloat16), 1, 0)

    over_blocks(plan, 4 * at, body)
    for h in range(heads):
        rows = pl.ds(h * head, head)
        value = out[rows, :] / total[pl.ds(h, 1), :]
        out[rows, :] = value
        out_low[rows, :] = value.astype(jnp.bfloat16)
    logsum[...] = best[...] + jnp.log(total[...]) * LOG2E


def backward_kernel(
    before, heads, head, plan, query, pair, start, grad, out, logsum, cosine, sine,
    query_grad, pair_grad, query_sum, pair_sum, delta,
):
    at = pl.program_id(0) * pl.num_programs(1) + pl.program_id(1)
    begin = before + pl.program_id(1) * query_block
    scale = head**-0.5

    @pl.when(pl.program_id(1) == 0)
    def _():
        pair_sum[...] = jnp.zeros(pair_sum.shape, jnp.float32)

    query_sum[...] = jnp.zeros(query_sum.shape, jnp.float32)
    for h in range(heads):
        rows = pl.ds(h * head, head)
        delta[pl.ds(h, 1), :] = jnp.sum(
            grad[rows, :].astype(jnp.float32) * out[rows, :], axis=0, keepdims=True
        )

    def body(block, masked):
        keys = pl.ds(pl.multiple_of(block * key_block, key_block), key_block)
        key_wide = pair[0, :head, keys]
        key = key_wide.T
        value = pair[0, head:, keys].T
        if masked:
            allowed = allowed_pairs(block, start[...], begin)
        key_grad = jnp.zeros((head, key_block), jnp.float32)
        value_grad = jnp.zeros((head, key_block), jnp.float32)
        for h in range(heads):
            rows = pl.ds(h * head, head)
            scores = dot(key, query[rows, :], 1, 0) * (scale * LOG2E)
            probs = jnp.exp2(scores - logsum[pl.ds(h, 1), :])
            if masked:
                probs = jnp.where(allowed, probs, 0.0)
            value_grad += dot(grad[rows, :], probs.astype(jnp.bfloat16), 1, 1)
            prob_grad = dot(value, grad[rows, :], 1, 0)
            score_grad = (probs * (prob_grad - delta[pl.ds(h, 1), :])).astype(jnp.bfloat16)
            query_sum[rows, :] += dot(key_wide, score_grad, 1, 0)
            key_grad += dot(query[rows, :], score_grad, 1, 1)
        pair_sum[:head, keys] += key_grad
        pair_sum[head:, keys] += value_grad

    over_blocks(plan, 4 * at, body)
    half = ROT // 2
    for h in range(heads):
        value = query_sum[pl.ds(h * head, head), :] * scale
        first, second = value[:half], value[half:ROT]
        turned = jnp.concatenate(
            [
                first * cosine[...] + second * sine[...],
                second * cosine[...] - first * sine[...],
                value[ROT:],
            ],
            axis=0,
        )
        query_grad[pl.ds(h * head, head), :] = turned.astype(jnp.bfloat16)

    @pl.when(pl.program_id(1) == pl.num_programs(1) - 1)
    def _():
        pair_grad[0, :head, :] = (pair_sum[:head, :] * scale).astype(jnp.bfloat16)
        pair_grad[0, head:, :] = pair_sum[head:, :].astype(jnp.bfloat16)


def attention_specs(heads, head, blocks, window):
    rows = heads * head
    query = pl.BlockSpec((rows, query_block), lambda m, i, plan: (0, m * blocks + i))
    pair = pl.BlockSpec((1, 2 * head, window), lambda m, i, plan: (m, 0, 0))
    single = pl.BlockSpec((1, query_block), lambda m, i, plan: (0, m * blocks + i))
    per_head = pl.BlockSpec((heads, query_block), lambda m, i, plan: (0, m * blocks + i))
    table = pl.BlockSpec((ROT // 2, query_block), lambda m, i, plan: (0, m * blocks + i))
    return query, pair, single, per_head, table


def attention_cost(micro, rows, length, products):
    pairs = micro * (rows // 64) * length * 2 * length
    return pl.CostEstimate(
        flops=2 * products * 64 * pairs, bytes_accessed=8 * micro * rows * length, transcendentals=pairs
    )


def attend_forward(plan, query, pair, start, before, heads, head):
    micro, _, window = pair.shape
    rows, count = query.shape
    blocks = count // micro // query_block
    q_spec, pair_spec, single, per_head, _ = attention_specs(heads, head, blocks, window)
    return pl.pallas_call(
        functools.partial(forward_kernel, before, heads, head),
        grid_spec=pltpu.PrefetchScalarGridSpec(
            num_scalar_prefetch=1,
            grid=(micro, blocks),
            in_specs=[q_spec, pair_spec, single],
            out_specs=[q_spec, q_spec, per_head],
            scratch_shapes=[
                pltpu.VMEM((heads, query_block), jnp.float32),
                pltpu.VMEM((heads, query_block), jnp.float32),
            ],
        ),
        out_shape=[
            jax.ShapeDtypeStruct((rows, count), jnp.float32),
            jax.ShapeDtypeStruct((rows, count), jnp.bfloat16),
            jax.ShapeDtypeStruct((heads, count), jnp.float32),
        ],
        compiler_params=pltpu.CompilerParams(vmem_limit_bytes=32 << 20),
        cost_estimate=attention_cost(micro, rows, count // micro, 2),
        name="attend_forward",
    )(plan, query, pair, start)


def attend_backward(plan, query, pair, start, grad, out, logsum, cosine, sine, before, heads, head):
    micro, _, window = pair.shape
    rows, count = query.shape
    blocks = count // micro // query_block
    q_spec, pair_spec, single, per_head, table = attention_specs(heads, head, blocks, window)
    return pl.pallas_call(
        functools.partial(backward_kernel, before, heads, head),
        grid_spec=pltpu.PrefetchScalarGridSpec(
            num_scalar_prefetch=1,
            grid=(micro, blocks),
            in_specs=[q_spec, pair_spec, single, q_spec, q_spec, per_head, table, table],
            out_specs=[q_spec, pair_spec],
            scratch_shapes=[
                pltpu.VMEM((rows, query_block), jnp.float32),
                pltpu.VMEM((2 * head, window), jnp.float32),
                pltpu.VMEM((heads, query_block), jnp.float32),
            ],
        ),
        out_shape=[
            jax.ShapeDtypeStruct((rows, count), jnp.bfloat16),
            jax.ShapeDtypeStruct((micro, 2 * head, window), jnp.bfloat16),
        ],
        compiler_params=pltpu.CompilerParams(vmem_limit_bytes=32 << 20),
        cost_estimate=attention_cost(micro, rows, count // micro, 5),
        name="attend_backward",
    )(plan, query, pair, start, grad, out, logsum, cosine, sine)


def shards(
    tokens,
    segments,
    query_weight,
    query_bias,
    key_weight,
    key_bias,
    value_weight,
    value_bias,
    output_weight,
    output_bias,
    upward_weight,
    upward_bias,
    down_weight,
    down_bias,
    attend_gain,
    attend_bias,
    dense_gain,
    dense_bias,
    cotangent,
):
    low = jnp.bfloat16
    micro, _, length, width = tokens.shape
    count = micro * length
    head = key_weight.shape[1]
    query_width = query_bias.shape[0]
    heads = query_width // head
    hidden_width = upward_bias.shape[0]
    devices = lax.axis_size("fsdp") * lax.axis_size("ctx")
    reach = lax.axis_size("ctx") // 2
    before = reach * length
    window = before + length
    core = lax.axis_index("tp")
    stages = all_bits()
    deep = [s for s in stages if s[0] == "ctx" and s[1] > 1]
    near = [s for s in stages if s[0] == "ctx" and s[1] == 1]
    side = [s for s in stages if s[0] == "fsdp"]

    shard_rows = key_weight.shape[0]
    pad_rows = -shard_rows % 16
    segment_rows = count // LANES
    seg_pad = -segment_rows % 16
    pair_piece = jnp.concatenate([key_weight, value_weight], axis=1)
    segment_piece = (segments + 1).astype(low).reshape(segment_rows, LANES)
    first_piece = jnp.concatenate(
        [
            jnp.pad(pair_piece, ((0, pad_rows), (0, 0))),
            jnp.pad(segment_piece, ((0, seg_pad), (0, 0))),
        ]
    )
    first_all = gather_shards(first_piece, side + deep + near)
    w_pair = first_all[:, :shard_rows].reshape(width, 2 * head)
    segment_all = first_all[:, shard_rows + pad_rows :][:, :segment_rows].reshape(
        lax.axis_size("fsdp"), lax.axis_size("ctx"), micro, length
    )
    bulk = lax.all_gather(
        jnp.concatenate([query_weight, output_weight.T, upward_weight, down_weight.T], axis=1),
        SHARDED,
        axis=0,
        tiled=True,
    )
    cuts = [query_width, 2 * query_width, 2 * query_width + hidden_width]
    w_query, w_output, w_upward, w_down = jnp.split(bulk, cuts, axis=1)

    mine = lax.dynamic_index_in_dim(segment_all, lax.axis_index("fsdp"), 0, keepdims=False)
    padded = jnp.concatenate([jnp.zeros((reach,) + mine.shape[1:], low), mine])
    seen = lax.dynamic_slice_in_dim(padded, lax.axis_index("ctx"), reach + 1)
    seen = jnp.transpose(seen, (1, 0, 2)).reshape(micro, window).astype(jnp.int32)
    local = segments[:, 0] + 1
    start = jnp.sum((seen[:, None, :] < local[:, :, None]).astype(jnp.int32), axis=2)
    positions = (before + jnp.arange(length, dtype=jnp.int32))[None] - start
    freqs = jnp.exp(
        jnp.arange(ROT // 2, dtype=jnp.float32) * (-2.0 * math.log(10000.0) / ROT)
    )
    angle = freqs[:, None] * positions.reshape(1, count).astype(jnp.float32)
    cosine, sine = jnp.cos(angle), jnp.sin(angle)
    plan = block_plan(start, before, micro, length)
    start = start.reshape(1, count)

    inputs = tokens.reshape(count, width).astype(jnp.float32)
    normed, spread = norm_parts(inputs)
    attend_in = (normed * attend_gain + attend_bias).astype(low)
    dense_in = (normed * dense_gain + dense_bias).astype(low)

    split = micro % lax.axis_size("tp") == 0 and lax.axis_size("tp") == 2 and micro == 2
    pair_lin = dot(w_pair, attend_in, 0, 1) + jnp.concatenate([key_bias, value_bias])[:, None]
    pair_all = jnp.concatenate(
        [rotate(pair_lin[:head], cosine, sine), pair_lin[head:]], axis=0
    ).astype(low)
    assert split
    pair_mine = jnp.where(core == 0, pair_all[:, :length], pair_all[:, length:])
    context = lax.axis_size("ctx")
    parts = [pair_mine]
    for d in range(1, reach + 1):
        parts.append(lax.ppermute(pair_mine, "ctx", [(i, i + d) for i in range(context - d)]))
    pair_half = jnp.concatenate(parts[::-1], axis=1)
    pair_other = partner(pair_half, ("tp", 1))
    pair = jnp.stack(
        [jnp.where(core == 0, pair_half, pair_other), jnp.where(core == 0, pair_other, pair_half)]
    )

    query_lin = dot(w_query, attend_in, 0, 1) + query_bias[:, None]
    query = (
        rotate(query_lin.reshape(heads, head, count), cosine, sine)
        .astype(low)
        .reshape(query_width, count)
    )
    attended, attended_low, logsum = attend_forward(plan, query, pair, start, before, heads, head)

    grad_low = cotangent.reshape(count, width)
    grad_full = grad_low.astype(jnp.float32)
    hidden_pre = dot(dense_in, w_upward, 1, 0) + upward_bias
    normal_cdf = 0.5 * (1.0 + lax.erf(hidden_pre * (1.0 / math.sqrt(2.0))))
    normal_pdf = jnp.exp(-0.5 * hidden_pre * hidden_pre) * (1.0 / math.sqrt(2.0 * math.pi))
    hidden = (hidden_pre * normal_cdf).astype(low)
    slope = normal_cdf + hidden_pre * normal_pdf
    pre_grad = (dot(grad_low, w_down, 1, 0) * slope).astype(low)
    dense_part = dot(pre_grad, w_upward, 1, 1)

    def by_device(values):
        return values.astype(low).reshape(devices, shard_rows, values.shape[1])

    grad_up = scatter_sum(by_device(dot(dense_in, pre_grad, 0, 0)), side + near + deep[::-1])
    grad_down = scatter_sum(by_device(dot(grad_low, hidden, 0, 0)), near + side + deep[::-1])

    attended_grad = dot(w_output, grad_low, 0, 1).astype(low)
    query_grad, pair_back = attend_backward(
        plan, query, pair, start, attended_grad, attended, logsum, cosine, sine, before, heads, head
    )

    send = jnp.where(core == 0, pair_back[1], pair_back[0])
    keep = jnp.where(core == 0, pair_back[0], pair_back[1])
    summed = (
        keep.astype(jnp.float32) + partner(send, ("tp", 1)).astype(jnp.float32)
    ).astype(low)
    pair_sum = summed[:, before:].astype(jnp.float32)
    for d in range(1, reach + 1):
        piece = summed[:, before - d * length : before - (d - 1) * length]
        pair_sum = pair_sum + lax.ppermute(
            piece, "ctx", [(i + d, i) for i in range(context - d)]
        ).astype(jnp.float32)
    pair_half = pair_sum.astype(low)
    pair_other = partner(pair_half, ("tp", 1))
    pair_grad = jnp.concatenate(
        [jnp.where(core == 0, pair_half, pair_other), jnp.where(core == 0, pair_other, pair_half)],
        axis=1,
    ).astype(jnp.float32)
    pair_low = jnp.concatenate(
        [rotate(pair_grad[:head], cosine, -sine), pair_grad[head:]], axis=0
    ).astype(low)

    pair_low_half = jnp.where(core == 0, pair_low[:head], pair_low[head:])
    w_pair_half = jnp.where(core == 0, w_pair[:, :head], w_pair[:, head:])
    attend_part = dot(query_grad, w_query, 0, 1) + dot(pair_low_half, w_pair_half, 0, 1)
    norm_part = (attend_part * attend_gain + dense_part * dense_gain).astype(low)
    norm_grad = norm_part.astype(jnp.float32) + partner(norm_part, ("tp", 1)).astype(jnp.float32)
    tokens_grad = (
        grad_full
        + spread
        * (
            norm_grad
            - jnp.mean(norm_grad, axis=-1, keepdims=True)
            - normed * jnp.mean(norm_grad * normed, axis=-1, keepdims=True)
        )
    ).astype(low)

    branches = (dot(attended_low, w_output, 0, 1) + dot(hidden, w_down, 1, 1)).astype(low)
    mixed = branches.astype(jnp.float32) + partner(branches, ("tp", 1)).astype(jnp.float32)
    result = (inputs + mixed + output_bias + down_bias).astype(low)

    grad_out = scatter_sum(
        by_device(dot(grad_low, attended_low, 0, 1)), side + near + deep[::-1]
    )
    grad_in = jnp.concatenate(
        [dot(attend_in, query_grad, 0, 1), dot(attend_in, pair_low, 0, 1)], axis=1
    )
    grad_in = scatter_sum(by_device(grad_in), near + side + deep[::-1])

    shared = jnp.concatenate(
        [
            jnp.sum(attend_part * normed, axis=0),
            jnp.sum(attend_part, axis=0),
            jnp.sum(dense_part * normed, axis=0),
            jnp.sum(dense_part, axis=0),
        ]
    )
    shared = shared + partner(shared, ("tp", 1))
    small = jnp.concatenate(
        [
            shared,
            jnp.sum(grad_full, axis=0),
            jnp.sum(pre_grad.astype(jnp.float32), axis=0),
            jnp.sum(query_grad.astype(jnp.float32), axis=1),
            jnp.sum(pair_low.astype(jnp.float32), axis=1),
        ]
    )
    small = total_sum(small.reshape(-1, LANES), stages).reshape(-1)
    sizes = [width] * 5 + [hidden_width, query_width, head, head]
    bounds = [sum(sizes[: i + 1]) for i in range(len(sizes) - 1)]
    g_gain, g_shift, d_gain, d_shift, out_b, up_b, q_b, k_b, v_b = jnp.split(small, bounds)
    shape = (micro, 1, length, width)
    return (
        result.reshape(shape),
        tokens_grad.reshape(shape),
        grad_in[:, :query_width],
        q_b,
        grad_in[:, query_width : query_width + head],
        k_b,
        grad_in[:, query_width + head :],
        v_b,
        grad_out.T,
        out_b,
        grad_up,
        up_b,
        grad_down.T,
        out_b,
        g_gain,
        g_shift,
        d_gain,
        d_shift,
    )


def solution(mesh):
    return jax.shard_map(
        shards,
        mesh=mesh,
        in_specs=(
            P(None, "fsdp", "ctx", None),
            P(None, "fsdp", "ctx"),
            P(("fsdp", "ctx"), "tp"),
            P("tp"),
            P(("fsdp", "ctx"), None),
            P(),
            P(("fsdp", "ctx"), None),
            P(),
            P("tp", ("fsdp", "ctx")),
            P(),
            P(("fsdp", "ctx"), "tp"),
            P("tp"),
            P("tp", ("fsdp", "ctx")),
            P(),
            P(),
            P(),
            P(),
            P(),
            P(None, "fsdp", "ctx", None),
        ),
        out_specs=(
            P(None, "fsdp", "ctx", None),
            P(None, "fsdp", "ctx", None),
            P(("fsdp", "ctx"), "tp"),
            P("tp"),
            P(("fsdp", "ctx"), None),
            P(),
            P(("fsdp", "ctx"), None),
            P(),
            P("tp", ("fsdp", "ctx")),
            P(),
            P(("fsdp", "ctx"), "tp"),
            P("tp"),
            P("tp", ("fsdp", "ctx")),
            P(),
            P(),
            P(),
            P(),
            P(),
        ),
        check_vma=False,
    )
```

time: 1670 us -> 370 us (0.22)
  waiting for transfers between devices: 720 us -> 133 us
  matrix products: 347 us -> 31.8 us
  blocking collectives: 266 us -> 0 us
  starting transfers between devices: 0.74 us -> 120 us
  local copies, waits for them, and re-layouts: 113 us -> 15 us
  other arithmetic: 127 us -> 29.2 us
  loops' own time: 65 us -> 0 us
  Pallas kernels: 0 us -> 24.6 us
    reduce_scatter x6 -> x0, waiting for transfers between devices: 442 us -> none  [the longest x1 143 us: finish(): lax.psum_scatter(weight_terms[4], ('fsdp', 'ctx'), scatter_dimension=0, t...]
    dot_general x142 -> x15, matrix products: 347 us -> 31.8 us  [dot(): lax.dot_general(left, right, (((left_dim,), (right_dim,)), ((), ())), pre...]
    unnamed x15 -> x1, waiting for transfers between devices: 253 us -> 0.02 us
    all_gather x5 -> x0, blocking collectives: 188 us -> none  [the longest x1 42.2 us: shards(): lax.all_gather(query_weight, ('fsdp', 'ctx'), axis=0, tiled=True)]
    ppermute x0 -> x38, starting transfers between devices: none -> 120 us  [the longest x30 102 us: partner(): return lax.ppermute(values, name, pairs)]
    ppermute x0 -> x38, waiting for transfers between devices: none -> 83.4 us  [the longest x30 68.7 us: partner(): return lax.ppermute(values, name, pairs)]
    psum x1 -> x0, blocking collectives: 77.6 us -> none  [finish(): lax.psum((bias_terms[0], bias_terms[1], bias_terms[2], bias_terms[3], bia...]
    reduce_sum x27 -> x7, other arithmetic: 82.8 us -> 6.31 us  [the longest x1 2.14 us: shards(): jnp.mean(norm_grad, axis=-1, keepdims=True)]
  transfers between devices with their start and end apart: 13 -> 39, of which waited for: 8 -> 26; matrix products, arithmetic and copies ran while one was open for 34% -> 16% of each run, Pallas kernels for 0% -> 7%
where the time goes in v1:
time: 370 us; the launch traced here: 369 us
  waiting for transfers between devices  133 us (36%)
  starting transfers between devices  120 us (32%)
  matrix products  31.8 us (9%)
  other arithmetic  29.2 us (8%)
  Pallas kernels  24.6 us (7%)
  between operations  15.3 us (4%)
  local copies, waits for them, and re-layouts  15 us (4%)
    ppermute x30, starting transfers between devices, partner(): return lax.ppermute(values, name, pairs)  102 us
    ppermute x30, waiting for transfers between devices, partner(): return lax.ppermute(values, name, pairs)  68.7 us
    all_gather x1, waiting for transfers between devices, shards(): lax.all_gather(jnp.concatenate([query_weight, output_weight.T, upward_wei...  49.4 us
    dot_general x15, matrix products, dot(): lax.dot_general(left, right, (((left_dim,), (right_dim,)), ((), ())), pre...  31.8 us
    pallas_call x1, Pallas kernels, attend_backward(): pl.pallas_call(functools.partial(backward_kernel, before, heads, head), g...  12.9 us
    ppermute x4, starting transfers between devices, shards(): lax.ppermute(pair_mine, 'ctx', [(i, i + d) for i in range(context - d)])  12.2 us
    pallas_call x1, Pallas kernels, attend_forward(): pl.pallas_call(functools.partial(forward_kernel, before, heads, head), gr...  11.7 us
    ppermute x4, waiting for transfers between devices, shards(): lax.ppermute(piece, 'ctx', [(i + d, i) for i in range(context - d)])  10.1 us
  transfers between devices with their start and end apart: 39, of which 26 were waited for; matrix products, arithmetic and copies ran while one was open for 16% of the time, Pallas kernels for 7%

profile of v1, /device:TPU:0, one launch (start us, length us, event | category | flops | bytes accessed | tf_op | source)
XLA Modules:
  0.0 368.8 jit_solution(13115656581267330307)
XLA Ops:
  23.5 5.0 %collective-permute-done.2 = bf16[4,64,128]{2,1,0:T(8,128)(2,1)S(1)} collective-permute-done((bf16[4,64,128]{2,1,0:T(8,128)(2,1)S(1)}, bf16[4,64,128]{2,1,0:T(8,128)(2,1)S(1)}, u32[]{:S(2)}, u32[]{:S(2)}) %collective-permute-start.2) | collective-permute-done | bytes 65568 | tf_op jit(solution)/shard_map/ppermute | solution.py:41
  30.1 3.4 collective-permute-done.3
  39.3 4.6 %collective-permute-start.5 = (bf16[128,512]{1,0:T(8,128)(2,1)S(1)}, bf16[128,512]{1,0:T(8,128)(2,1)S(1)}, u32[]{:S(2)}, u32[]{:S(2)}) collective-permute-start(bf16[128,512]{1,0:T(8,128)(2,1)S(1)} %slice_select_fusion.2), channel_id=1, source_target_pairs={{0,6},{2,8},{4,10},{6,12},{8,14},{1,7},{3,9},{5,11},{7,13},{9,15},... | collective-permute-start | bytes 393224 | tf_op jit(solution)/shard_map/ppermute | solution.py:409
  51.0 3.5 collective-permute-done.6
  62.4 49.4 %all-gather.2.cloned.1.call-done = bf16[768,3840]{1,0:T(8,128)(2,1)} async-done(((bf16[48,3840]{1,0:T(8,128)(2,1)}), bf16[768,3840]{1,0:T(8,128)(2,1)}) %all-gather.2.cloned.1.call-update) | async-done | bytes 5898256 | tf_op jit(solution)/shard_map/all_gather | solution.py:370
  111.8 5.1 %multiply_convert_fusion = (bf16[1024,1536]{1,0:T(8,128)(2,1)S(1)}, f32[1024,1536]{1,0:T(8,128)S(1)}) fusion(f32[1536]{0:T(1024)S(1)} %copy-done.26, bf16[1024,768]{1,0:T(8,128)(2,1)} %get-tuple-element.136, bf16[768,3840]{1,0:T(8,128)(2,1)} %all-gather.2.cloned.1.call-done), kind=kOutput, calls=%fused_computation.9 | convolution fusion | flops 2425356288 | bytes 13375488 | tf_op jit(solution)/shard_map/dot_general | solution.py:22
  124.0 5.6 %convert_reduce_fusion.1 = (f32[1536]{0:T(1024)S(1)}, bf16[1024,1536]{1,0:T(8,128)(2,1)S(1)}) fusion(f32[1024,1536]{1,0:T(8,128)S(1)} %get-tuple-element.179, f32[1536]{0:T(1024)S(1)} %copy-done.26, bf16[1024,768]{1,0:T(8,128)(2,1)S(1)} %bitcast.468, bf16[768,3840]{1,0:T(8,128)(2,1)S(1)} %copy-done.15), kind=kOutput, calls=%fused_computation.8 | convolution fusion | flops 2436364800 | bytes 13383680 | tf_op jit(solution)/shard_map/dot_general | solution.py:22
  135.0 11.7 %attend_forward.1 = (f32[384,1024]{1,0:T(8,128)S(1)}, bf16[384,1024]{1,0:T(8,128)(2,1)S(1)}, f32[6,1024]{1,0:T(8,128)S(1)}) custom-call(s32[16]{0:T(128)S(1)} %reshape.1034.plan, bf16[384,1024]{1,0:T(8,128)(2,1)S(1)} %bitcast.450, bf16[2,128,2560]{2,1,0:T(8,128)(2,1)S(1)} %pad_maximum_fusion.pair, s32[1,1024]{1,0:T(1,128)S(1)} %bitcast.452), custom_call_target="tpu_custom_call" | custom-call | flops 1610612736 | bytes 3145728 | tf_op jit(solution)/shard_map/attend_forward/pallas_call | solution.py:264
  156.0 12.9 %attend_backward.1 = (bf16[384,1024]{1,0:T(8,128)(2,1)S(1)}, bf16[2,128,2560]{2,1,0:T(8,128)(2,1)S(1)}) custom-call(s32[16]{0:T(128)S(1)} %reshape.1034.plan, bf16[384,1024]{1,0:T(8,128)(2,1)S(1)} %bitcast.451, bf16[2,128,2560]{2,1,0:T(8,128)(2,1)S(1)} %pad_maximum_fusion.pair, s32[1,1024]{1,0:T(1,128)S(1)} %bitcast.453, ...), custom_call_target="tpu_custom_call" | custom-call | flops 4026531840 | bytes 3145728 | tf_op jit(solution)/shard_map/attend_backward/pallas_call | solution.py:292
  173.0 14.3 %collective-permute-start.27 = (bf16[4,48,384]{2,1,0:T(8,128)(2,1)S(1)}, bf16[4,48,384]{2,1,0:T(8,128)(2,1)S(1)}, u32[]{:S(2)}, u32[]{:S(2)}) collective-permute-start(bf16[4,48,384]{2,1,0:T(8,128)(2,1)S(1)} %select_bitcast_fusion.9), channel_id=1, source_target_pairs={{0,2},{2,0},{4,6},{6,4},{8,10},{10,8},{12,14},{14,12},{1,3},{3,1},... | collective-permute-start | bytes 442376 | tf_op jit(solution)/shard_map/ppermute | solution.py:41
  188.2 3.5 collective-permute-done.27
  191.8 50.6 %collective-permute-start.28 = (bf16[2,48,384]{2,1,0:T(8,128)(2,1)S(1)}, bf16[2,48,384]{2,1,0:T(8,128)(2,1)S(1)}, u32[]{:S(2)}, u32[]{:S(2)}) collective-permute-start(bf16[2,48,384]{2,1,0:T(8,128)(2,1)S(1)} %fusion.89), channel_id=1, source_target_pairs={{0,4},{2,6},{4,0},{6,2},{8,12},{10,14},{12,8},{14,10},{1,5},{3,7},... | collective-permute-start | bytes 221192 | tf_op jit(solution)/shard_map/ppermute | solution.py:41
  251.9 3.8 %collective-permute-done.12 = bf16[128,512]{1,0:T(8,128)(2,1)S(1)} collective-permute-done((bf16[128,512]{1,0:T(8,128)(2,1)S(1)}, bf16[128,512]{1,0:T(8,128)(2,1)S(1)}, u32[]{:S(2)}, u32[]{:S(2)}) %collective-permute-start.12) | collective-permute-done | bytes 131104 | tf_op jit(solution)/shard_map/ppermute | solution.py:453
  257.8 12.1 %collective-permute-start.29 = (bf16[1,48,384]{2,1,0:T(8,128)(2,1)S(1)}, bf16[1,48,384]{2,1,0:T(8,128)(2,1)S(1)}, u32[]{:S(2)}, u32[]{:S(2)}) collective-permute-start(bf16[1,48,384]{2,1,0:T(8,128)(2,1)S(1)} %fusion.102), channel_id=1, source_target_pairs={{0,8},{2,10},{4,12},{6,14},{8,0},{10,2},{12,4},{14,6},{1,9},{3,11}... | collective-permute-start | bytes 110600 | tf_op jit(solution)/shard_map/ppermute | solution.py:41
  285.6 8.0 %collective-permute-done.17 = bf16[8,48,512]{2,1,0:T(8,128)(2,1)S(1)} collective-permute-done((bf16[8,48,512]{2,1,0:T(8,128)(2,1)S(1)}, bf16[8,48,512]{2,1,0:T(8,128)(2,1)S(1)}, u32[]{:S(2)}, u32[]{:S(2)}) %collective-permute-start.17) | collective-permute-done | bytes 393248 | tf_op jit(solution)/shard_map/ppermute | solution.py:41
  293.9 4.5 %collective-permute-start.18 = (bf16[4,48,512]{2,1,0:T(8,128)(2,1)S(1)}, bf16[4,48,512]{2,1,0:T(8,128)(2,1)S(1)}, u32[]{:S(2)}, u32[]{:S(2)}) collective-permute-start(bf16[4,48,512]{2,1,0:T(8,128)(2,1)S(1)} %select_bitcast_fusion.7), channel_id=1, source_target_pairs={{0,16},{16,0},{1,17},{17,1},{2,18},{18,2},{3,19},{19,3},{4,20},{20... | collective-permute-start | bytes 589832 | tf_op jit(solution)/shard_map/ppermute | solution.py:41
  298.5 5.6 %collective-permute-done.18 = bf16[4,48,512]{2,1,0:T(8,128)(2,1)S(1)} collective-permute-done((bf16[4,48,512]{2,1,0:T(8,128)(2,1)S(1)}, bf16[4,48,512]{2,1,0:T(8,128)(2,1)S(1)}, u32[]{:S(2)}, u32[]{:S(2)}) %collective-permute-start.18) | collective-permute-done | bytes 196640 | tf_op jit(solution)/shard_map/ppermute | solution.py:41
  304.7 4.1 %collective-permute-done.19 = bf16[2,48,512]{2,1,0:T(8,128)(2,1)S(1)} collective-permute-done((bf16[2,48,512]{2,1,0:T(8,128)(2,1)S(1)}, bf16[2,48,512]{2,1,0:T(8,128)(2,1)S(1)}, u32[]{:S(2)}, u32[]{:S(2)}) %collective-permute-start.19) | collective-permute-done | bytes 98336 | tf_op jit(solution)/shard_map/ppermute | solution.py:41
  316.4 5.8 %collective-permute-done.31 = bf16[4,48,1536]{2,1,0:T(8,128)(2,1)S(1)} collective-permute-done((bf16[4,48,1536]{2,1,0:T(8,128)(2,1)S(1)}, bf16[4,48,1536]{2,1,0:T(8,128)(2,1)S(1)}, u32[]{:S(2)}, u32[]{:S(2)}) %collective-permute-start.31) | collective-permute-done | bytes 589856 | tf_op jit(solution)/shard_map/ppermute | solution.py:41
  322.8 3.5 collective-permute-done.36
  326.5 7.1 %collective-permute-done.32 = bf16[2,48,1536]{2,1,0:T(8,128)(2,1)S(1)} collective-permute-done((bf16[2,48,1536]{2,1,0:T(8,128)(2,1)S(1)}, bf16[2,48,1536]{2,1,0:T(8,128)(2,1)S(1)}, u32[]{:S(2)}, u32[]{:S(2)}) %collective-permute-start.32) | collective-permute-done | bytes 294944 | tf_op jit(solution)/shard_map/ppermute | solution.py:41
  336.2 4.3 %collective-permute-done.33 = bf16[1,48,1536]{2,1,0:T(8,128)(2,1)S(1)} collective-permute-done((bf16[1,48,1536]{2,1,0:T(8,128)(2,1)S(1)}, bf16[1,48,1536]{2,1,0:T(8,128)(2,1)S(1)}, u32[]{:S(2)}, u32[]{:S(2)}) %collective-permute-start.33) | collective-permute-done | bytes 147488 | tf_op jit(solution)/shard_map/ppermute | solution.py:41
  345.6 4.7 %collective-permute-done.23 = f32[46,128]{1,0:T(8,128)S(1)} collective-permute-done((f32[46,128]{1,0:T(8,128)S(1)}, f32[46,128]{1,0:T(8,128)S(1)}, u32[]{:S(2)}, u32[]{:S(2)}) %collective-permute-start.23) | collective-permute-done | bytes 23584 | tf_op jit(solution)/shard_map/ppermute | solution.py:41
  350.4 3.8 %collective-permute-done.24 = f32[46,128]{1,0:T(8,128)S(1)} collective-permute-done((f32[46,128]{1,0:T(8,128)S(1)}, f32[46,128]{1,0:T(8,128)S(1)}, u32[]{:S(2)}, u32[]{:S(2)}) %collective-permute-start.24) | collective-permute-done | bytes 23584 | tf_op jit(solution)/shard_map/ppermute | solution.py:41
  (273 shorter events, 116.6 us)
Async XLA Ops:
  7.2 104.6 %all-gather.2.cloned.1.call-start = ((), (), s32[]{:S(2)}) async-start(), calls=%async_computation | async-start | bytes 6266880 | tf_op jit(solution)/shard_map/all_gather | solution.py:370
  36.1 12.3 %collective-permute-start.4 = (bf16[128,512]{1,0:T(8,128)(2,1)S(1)}, bf16[128,512]{1,0:T(8,128)(2,1)S(1)}, u32[]{:S(2)}, u32[]{:S(2)}) collective-permute-start(bf16[128,512]{1,0:T(8,128)(2,1)S(1)} %slice_select_fusion.2), channel_id=1, source_target_pairs={{0,8},{2,10},{4,12},{6,14},{1,9},{3,11},{5,13},{7,15},{16,24},{18,... | collective-permute-start | bytes 393224 | tf_op jit(solution)/shard_map/ppermute | solution.py:409
  39.3 10.9 %collective-permute-start.5 = (bf16[128,512]{1,0:T(8,128)(2,1)S(1)}, bf16[128,512]{1,0:T(8,128)(2,1)S(1)}, u32[]{:S(2)}, u32[]{:S(2)}) collective-permute-start(bf16[128,512]{1,0:T(8,128)(2,1)S(1)} %slice_select_fusion.2), channel_id=1, source_target_pairs={{0,6},{2,8},{4,10},{6,12},{8,14},{1,7},{3,9},{5,11},{7,13},{9,15},... | collective-permute-start | bytes 393224 | tf_op jit(solution)/shard_map/ppermute | solution.py:409
  44.0 10.5 %collective-permute-start.6 = (bf16[128,512]{1,0:T(8,128)(2,1)S(1)}, bf16[128,512]{1,0:T(8,128)(2,1)S(1)}, u32[]{:S(2)}, u32[]{:S(2)}) collective-permute-start(bf16[128,512]{1,0:T(8,128)(2,1)S(1)} %slice_select_fusion.2), channel_id=1, source_target_pairs={{0,4},{2,6},{4,8},{6,10},{8,12},{10,14},{1,5},{3,7},{5,9},{7,11},{... | collective-permute-start | bytes 393224 | tf_op jit(solution)/shard_map/ppermute | solution.py:409
  45.3 9.9 %collective-permute-start.7 = (bf16[128,512]{1,0:T(8,128)(2,1)S(1)}, bf16[128,512]{1,0:T(8,128)(2,1)S(1)}, u32[]{:S(2)}, u32[]{:S(2)}) collective-permute-start(bf16[128,512]{1,0:T(8,128)(2,1)S(1)} %slice_select_fusion.2), channel_id=1, source_target_pairs={{0,2},{2,4},{4,6},{6,8},{8,10},{10,12},{12,14},{1,3},{3,5},{5,7},{... | collective-permute-start | bytes 393224 | tf_op jit(solution)/shard_map/ppermute | solution.py:409
  122.4 161.5 %collective-permute-start.34 = (bf16[8,48,1536]{2,1,0:T(8,128)(2,1)}, bf16[8,48,1536]{2,1,0:T(8,128)(2,1)}, u32[]{:S(2)}, u32[]{:S(2)}) collective-permute-start(bf16[8,48,1536]{2,1,0:T(8,128)(2,1)} %fusion.46), channel_id=1, source_target_pairs={{0,2},{2,0},{4,6},{6,4},{8,10},{10,8},{12,14},{14,12},{1,3},{3,1},... | collective-permute-start | bytes 3538952 | tf_op jit(solution)/shard_map/ppermute | solution.py:41
  152.8 20.0 %collective-permute-start.26 = (bf16[8,48,384]{2,1,0:T(8,128)(2,1)S(1)}, bf16[8,48,384]{2,1,0:T(8,128)(2,1)S(1)}, u32[]{:S(2)}, u32[]{:S(2)}) collective-permute-start(bf16[8,48,384]{2,1,0:T(8,128)(2,1)S(1)} %select_bitcast_fusion.6), channel_id=1, source_target_pairs={{0,16},{16,0},{1,17},{17,1},{2,18},{18,2},{3,19},{19,3},{4,20},{20... | collective-permute-start | bytes 884744 | tf_op jit(solution)/shard_map/ppermute | solution.py:41
  169.0 75.8 %collective-permute-start.10 = (bf16[128,2560]{1,0:T(8,128)(2,1)S(1)}, bf16[128,2560]{1,0:T(8,128)(2,1)S(1)}, u32[]{:S(2)}, u32[]{:S(2)}) collective-permute-start(bf16[128,2560]{1,0:T(8,128)(2,1)S(1)} %select_bitcast_fusion.1), channel_id=1, source_target_pairs={{0,1},{1,0},{2,3},{3,2},{4,5},{5,4},{6,7},{7,6},{8,9},{9,8},{10,11... | collective-permute-start | bytes 1966088 | tf_op jit(solution)/shard_map/ppermute | solution.py:41
  173.0 18.7 %collective-permute-start.27 = (bf16[4,48,384]{2,1,0:T(8,128)(2,1)S(1)}, bf16[4,48,384]{2,1,0:T(8,128)(2,1)S(1)}, u32[]{:S(2)}, u32[]{:S(2)}) collective-permute-start(bf16[4,48,384]{2,1,0:T(8,128)(2,1)S(1)} %select_bitcast_fusion.9), channel_id=1, source_target_pairs={{0,2},{2,0},{4,6},{6,4},{8,10},{10,8},{12,14},{14,12},{1,3},{3,1},... | collective-permute-start | bytes 442376 | tf_op jit(solution)/shard_map/ppermute | solution.py:41
  191.8 53.0 %collective-permute-start.28 = (bf16[2,48,384]{2,1,0:T(8,128)(2,1)S(1)}, bf16[2,48,384]{2,1,0:T(8,128)(2,1)S(1)}, u32[]{:S(2)}, u32[]{:S(2)}) collective-permute-start(bf16[2,48,384]{2,1,0:T(8,128)(2,1)S(1)} %fusion.89), channel_id=1, source_target_pairs={{0,4},{2,6},{4,0},{6,2},{8,12},{10,14},{12,8},{14,10},{1,5},{3,7},... | collective-permute-start | bytes 221192 | tf_op jit(solution)/shard_map/ppermute | solution.py:41
  246.4 9.3 %collective-permute-start.12 = (bf16[128,512]{1,0:T(8,128)(2,1)S(1)}, bf16[128,512]{1,0:T(8,128)(2,1)S(1)}, u32[]{:S(2)}, u32[]{:S(2)}) collective-permute-start(bf16[128,512]{1,0:T(8,128)(2,1)S(1)} %get-tuple-element.144), channel_id=1, source_target_pairs={{4,0},{6,2},{8,4},{10,6},{12,8},{14,10},{5,1},{7,3},{9,5},{11,7},{... | collective-permute-start | bytes 393224 | tf_op jit(solution)/shard_map/ppermute | solution.py:453
  247.7 10.2 %collective-permute-start.13 = (bf16[128,512]{1,0:T(8,128)(2,1)S(1)}, bf16[128,512]{1,0:T(8,128)(2,1)S(1)}, u32[]{:S(2)}, u32[]{:S(2)}) collective-permute-start(bf16[128,512]{1,0:T(8,128)(2,1)S(1)} %get-tuple-element.143), channel_id=1, source_target_pairs={{6,0},{8,2},{10,4},{12,6},{14,8},{7,1},{9,3},{11,5},{13,7},{15,9},... | collective-permute-start | bytes 393224 | tf_op jit(solution)/shard_map/ppermute | solution.py:453
  249.0 23.8 %collective-permute-start.14 = (bf16[128,512]{1,0:T(8,128)(2,1)S(1)}, bf16[128,512]{1,0:T(8,128)(2,1)S(1)}, u32[]{:S(2)}, u32[]{:S(2)}) collective-permute-start(bf16[128,512]{1,0:T(8,128)(2,1)S(1)} %get-tuple-element.142), channel_id=1, source_target_pairs={{8,0},{10,2},{12,4},{14,6},{9,1},{11,3},{13,5},{15,7},{24,16},{26,... | collective-permute-start | bytes 393224 | tf_op jit(solution)/shard_map/ppermute | solution.py:453
  251.9 52.3 %collective-permute-start.30 = (bf16[8,48,1536]{2,1,0:T(8,128)(2,1)S(1)}, bf16[8,48,1536]{2,1,0:T(8,128)(2,1)S(1)}, u32[]{:S(2)}, u32[]{:S(2)}) collective-permute-start(bf16[8,48,1536]{2,1,0:T(8,128)(2,1)S(1)} %copy-done.14), channel_id=1, source_target_pairs={{0,16},{16,0},{1,17},{17,1},{2,18},{18,2},{3,19},{19,3},{4,20},{20... | collective-permute-start | bytes 3538952 | tf_op jit(solution)/shard_map/ppermute | solution.py:41
  255.7 99.8 %collective-permute-start.9 = (bf16[1024,768]{1,0:T(8,128)(2,1)S(1)}, bf16[1024,768]{1,0:T(8,128)(2,1)S(1)}, u32[]{:S(2)}, u32[]{:S(2)}) collective-permute-start(bf16[1024,768]{1,0:T(8,128)(2,1)S(1)} %add_convert_fusion.1), channel_id=1, source_target_pairs={{0,1},{1,0},{2,3},{3,2},{4,5},{5,4},{6,7},{7,6},{8,9},{9,8},{10,11... | collective-permute-start | bytes 4718600 | tf_op jit(solution)/shard_map/ppermute | solution.py:41
  257.8 15.4 %collective-permute-start.29 = (bf16[1,48,384]{2,1,0:T(8,128)(2,1)S(1)}, bf16[1,48,384]{2,1,0:T(8,128)(2,1)S(1)}, u32[]{:S(2)}, u32[]{:S(2)}) collective-permute-start(bf16[1,48,384]{2,1,0:T(8,128)(2,1)S(1)} %fusion.102), channel_id=1, source_target_pairs={{0,8},{2,10},{4,12},{6,14},{8,0},{10,2},{12,4},{14,6},{1,9},{3,11}... | collective-permute-start | bytes 110600 | tf_op jit(solution)/shard_map/ppermute | solution.py:41
  280.0 53.9 %collective-permute-start.16 = (bf16[1024,768]{1,0:T(8,128)(2,1)S(1)}, bf16[1024,768]{1,0:T(8,128)(2,1)S(1)}, u32[]{:S(2)}, u32[]{:S(2)}) collective-permute-start(bf16[1024,768]{1,0:T(8,128)(2,1)S(1)} %get-tuple-element.176), channel_id=1, source_target_pairs={{0,1},{1,0},{2,3},{3,2},{4,5},{5,4},{6,7},{7,6},{8,9},{9,8},{10,11... | collective-permute-start | bytes 4718600 | tf_op jit(solution)/shard_map/ppermute | solution.py:41
  280.9 12.8 %collective-permute-start.17 = (bf16[8,48,512]{2,1,0:T(8,128)(2,1)S(1)}, bf16[8,48,512]{2,1,0:T(8,128)(2,1)S(1)}, u32[]{:S(2)}, u32[]{:S(2)}) collective-permute-start(bf16[8,48,512]{2,1,0:T(8,128)(2,1)S(1)} %fusion.62), channel_id=1, source_target_pairs={{0,2},{2,0},{4,6},{6,4},{8,10},{10,8},{12,14},{14,12},{1,3},{3,1},... | collective-permute-start | bytes 1179656 | tf_op jit(solution)/shard_map/ppermute | solution.py:41
  293.9 10.2 %collective-permute-start.18 = (bf16[4,48,512]{2,1,0:T(8,128)(2,1)S(1)}, bf16[4,48,512]{2,1,0:T(8,128)(2,1)S(1)}, u32[]{:S(2)}, u32[]{:S(2)}) collective-permute-start(bf16[4,48,512]{2,1,0:T(8,128)(2,1)S(1)} %select_bitcast_fusion.7), channel_id=1, source_target_pairs={{0,16},{16,0},{1,17},{17,1},{2,18},{18,2},{3,19},{19,3},{4,20},{20... | collective-permute-start | bytes 589832 | tf_op jit(solution)/shard_map/ppermute | solution.py:41
  298.4 17.6 %collective-permute-start.35 = (bf16[4,48,1536]{2,1,0:T(8,128)(2,1)S(1)}, bf16[4,48,1536]{2,1,0:T(8,128)(2,1)S(1)}, u32[]{:S(2)}, u32[]{:S(2)}) collective-permute-start(bf16[4,48,1536]{2,1,0:T(8,128)(2,1)S(1)} %select_bitcast_fusion.4), channel_id=1, source_target_pairs={{0,16},{16,0},{1,17},{17,1},{2,18},{18,2},{3,19},{19,3},{4,20},{20... | collective-permute-start | bytes 1769480 | tf_op jit(solution)/shard_map/ppermute | solution.py:41
  309.1 13.1 %collective-permute-start.31 = (bf16[4,48,1536]{2,1,0:T(8,128)(2,1)S(1)}, bf16[4,48,1536]{2,1,0:T(8,128)(2,1)S(1)}, u32[]{:S(2)}, u32[]{:S(2)}) collective-permute-start(bf16[4,48,1536]{2,1,0:T(8,128)(2,1)S(1)} %fusion.53), channel_id=1, source_target_pairs={{0,2},{2,0},{4,6},{6,4},{8,10},{10,8},{12,14},{14,12},{1,3},{3,1},... | collective-permute-start | bytes 1769480 | tf_op jit(solution)/shard_map/ppermute | solution.py:41
  316.3 10.0 %collective-permute-start.36 = (bf16[2,48,1536]{2,1,0:T(8,128)(2,1)S(1)}, bf16[2,48,1536]{2,1,0:T(8,128)(2,1)S(1)}, u32[]{:S(2)}, u32[]{:S(2)}) collective-permute-start(bf16[2,48,1536]{2,1,0:T(8,128)(2,1)S(1)} %select_bitcast_fusion.5), channel_id=1, source_target_pairs={{0,4},{2,6},{4,0},{6,2},{8,12},{10,14},{12,8},{14,10},{1,5},{3,7},... | collective-permute-start | bytes 884744 | tf_op jit(solution)/shard_map/ppermute | solution.py:41
  322.4 11.2 %collective-permute-start.32 = (bf16[2,48,1536]{2,1,0:T(8,128)(2,1)S(1)}, bf16[2,48,1536]{2,1,0:T(8,128)(2,1)S(1)}, u32[]{:S(2)}, u32[]{:S(2)}) collective-permute-start(bf16[2,48,1536]{2,1,0:T(8,128)(2,1)S(1)} %fusion.66), channel_id=1, source_target_pairs={{0,4},{2,6},{4,0},{6,2},{8,12},{10,14},{12,8},{14,10},{1,5},{3,7},... | collective-permute-start | bytes 884744 | tf_op jit(solution)/shard_map/ppermute | solution.py:41
  326.4 17.4 %collective-permute-start.37 = (bf16[1,48,1536]{2,1,0:T(8,128)(2,1)S(1)}, bf16[1,48,1536]{2,1,0:T(8,128)(2,1)S(1)}, u32[]{:S(2)}, u32[]{:S(2)}) collective-permute-start(bf16[1,48,1536]{2,1,0:T(8,128)(2,1)S(1)} %select_bitcast_fusion.8), channel_id=1, source_target_pairs={{0,8},{2,10},{4,12},{6,14},{8,0},{10,2},{12,4},{14,6},{1,9},{3,11}... | collective-permute-start | bytes 442376 | tf_op jit(solution)/shard_map/ppermute | solution.py:41
  (51 other events, 515.4 us)
Sparse Core Ops, SparseCore 0:
  10.7 101.0 all-gather.1

commit v2 on v1

v2 whole, which is shorter than its diff:
```python
import functools
import math

import jax
import jax.numpy as jnp
from jax import lax
from jax.experimental import pallas as pl
from jax.experimental.pallas import tpu as pltpu
from jax.sharding import PartitionSpec as P

ROT = 16
NEGATIVE = -1e30
EPSILON = 1e-05
LOG2E = math.log2(math.e)
LANES = 128
forward_blocks = (512, 512)
backward_blocks = (256, 256)


def dot(left, right, left_dim, right_dim):
    return lax.dot_general(
        left,
        right,
        (((left_dim,), (right_dim,)), ((), ())),
        preferred_element_type=jnp.float32,
    )


def axis_bits(name):
    return [1 << b for b in reversed(range(lax.axis_size(name).bit_length() - 1))]


def all_bits():
    return [("fsdp", d) for d in axis_bits("fsdp")] + [("ctx", d) for d in axis_bits("ctx")]


def partner(values, stage):
    name, distance = stage
    pairs = [(i, i ^ distance) for i in range(lax.axis_size(name))]
    return lax.ppermute(values, name, pairs)


def own_bit(stage):
    name, distance = stage
    return (lax.axis_index(name) // distance) % 2 == 1


def gather_step(state, stage):
    held, done = state
    rank = {other: i for i, other in enumerate(all_bits())}
    low = 1 << sum(rank[other] > rank[stage] for other in done)
    piece = held.shape[1:]
    split = held.reshape((held.shape[0] // low, 1, low) + piece)
    other = partner(held, stage).reshape(split.shape)
    upper = own_bit(stage)
    held = jnp.concatenate(
        [jnp.where(upper, other, split), jnp.where(upper, split, other)], axis=1
    ).reshape((2 * held.shape[0],) + piece)
    return held, done + [stage]


def scatter_halves(held, left, stage):
    rank = {other: i for i, other in enumerate(all_bits())}
    low = 1 << sum(rank[other] > rank[stage] for other in left if other != stage)
    piece = held.shape[1:]
    split = held.reshape((held.shape[0] // (2 * low), 2, low) + piece)
    upper = own_bit(stage)
    shape = (held.shape[0] // 2,) + piece
    send = jnp.where(upper, split[:, 0], split[:, 1]).reshape(shape)
    keep = jnp.where(upper, split[:, 1], split[:, 0]).reshape(shape)
    return send, keep


def scatter_step(state, stage):
    held, left = state
    send, keep = scatter_halves(held, left, stage)
    left = [other for other in left if other != stage]
    total = keep.astype(jnp.float32) + partner(send, stage).astype(jnp.float32)
    return (total.astype(jnp.bfloat16) if left else total), left


def after(values, *others):
    return lax.optimization_barrier((values,) + others)[0]


def norm_parts(values):
    centre = values - jnp.mean(values, axis=-1, keepdims=True)
    spread = lax.rsqrt(jnp.mean(centre * centre, axis=-1, keepdims=True) + EPSILON)
    return centre * spread, spread


def rotate(values, cosine, sine):
    half = ROT // 2
    first = values[..., :half, :]
    second = values[..., half:ROT, :]
    return jnp.concatenate(
        [first * cosine - second * sine, second * cosine + first * sine, values[..., ROT:, :]],
        axis=-2,
    )


def block_plan(start, before, length, query_block, key_block):
    first = start[:, ::query_block]
    last = start[:, query_block - 1 :: query_block]
    begin = before + query_block * jnp.arange(length // query_block, dtype=jnp.int32)[None]
    lo = first // key_block
    hi = jnp.broadcast_to((begin + query_block - 1) // key_block + 1, lo.shape)
    a = jnp.clip((last + key_block - 1) // key_block, lo, hi)
    b = jnp.clip((begin + 1) // key_block, a, hi)
    return jnp.stack([lo, hi, a, b], axis=-1)


def allowed_pairs(block, key_block, start, last):
    key_index = block * key_block + lax.broadcasted_iota(
        jnp.int32, (key_block, start.shape[1]), 0
    )
    return (key_index >= start) & (key_index <= last)


def over_blocks(plan, at, body):
    lo, hi, a, b = plan[at], plan[at + 1], plan[at + 2], plan[at + 3]

    def step(block, carry):
        inside = (block >= a) & (block < b)

        @pl.when(inside)
        def _():
            body(block, False)

        @pl.when(jnp.logical_not(inside))
        def _():
            body(block, True)

        return carry

    lax.fori_loop(lo, hi, step, 0)


def spread_heads(pairs, heads, head, block):
    for h in range(heads):
        for wide, tall in pairs:
            wide[:, pl.ds(h * block, block)] = tall[pl.ds(h * head, head), :]


def forward_kernel(
    before, heads, head, key_block, plan, query, pair, start, out, out_low, logsum,
    wide, best, total, accum, first, last,
):
    block_rows = query.shape[1]
    at = pl.program_id(0) * pl.num_programs(1) + pl.program_id(1)
    begin = before + pl.program_id(1) * block_rows
    factor = head**-0.5 * LOG2E
    best[...] = jnp.full(best.shape, NEGATIVE, jnp.float32)
    total[...] = jnp.zeros(total.shape, jnp.float32)
    accum[...] = jnp.zeros(accum.shape, jnp.float32)
    spread_heads([(wide, query)], heads, head, block_rows)
    index = begin + lax.broadcasted_iota(jnp.int32, (1, block_rows), 1)
    for h in range(heads):
        first[:, pl.ds(h * block_rows, block_rows)] = start[...]
        last[:, pl.ds(h * block_rows, block_rows)] = index

    def body(block, masked):
        keys = pl.ds(pl.multiple_of(block * key_block, key_block), key_block)
        key = pair[0, :head, keys].T
        value = pair[0, head:, keys]
        value = jnp.concatenate([value, jnp.ones((8, key_block), jnp.bfloat16)], axis=0)
        scores = dot(key, wide[...], 1, 0) * factor
        if masked:
            allowed = allowed_pairs(block, key_block, first[...], last[...])
            scores = jnp.where(allowed, scores, NEGATIVE)
        old = best[...]
        fresh = jnp.maximum(old, jnp.max(scores, axis=0, keepdims=True))
        weights = jnp.exp2(scores - fresh).astype(jnp.bfloat16)
        shrink = jnp.exp2(old - fresh)
        best[...] = fresh
        product = dot(value, weights, 1, 0)
        accum[...] = accum[...] * shrink + product[:head]
        total[...] = total[...] * shrink + product[head : head + 1]

    over_blocks(plan, 4 * at, body)
    scaled = accum[...] / total[...]
    sums = best[...] + jnp.log(total[...]) * LOG2E
    for h in range(heads):
        columns = slice(h * block_rows, (h + 1) * block_rows)
        rows = pl.ds(h * head, head)
        out[rows, :] = scaled[:, columns]
        out_low[rows, :] = scaled[:, columns].astype(jnp.bfloat16)
        logsum[pl.ds(h, 1), :] = sums[:, columns]


def backward_kernel(
    before, heads, head, key_block, plan, query, pair, start, grad, out, logsum, cosine, sine,
    query_grad, pair_grad,
    wide, wide_grad, query_sum, pair_sum, sums, delta, first, last,
):
    block_rows = query.shape[1]
    begin = before + pl.program_id(0) * block_rows
    scale = head**-0.5

    @pl.when(pl.program_id(0) == 0)
    def _():
        pair_sum[...] = jnp.zeros(pair_sum.shape, jnp.float32)

    query_sum[...] = jnp.zeros(query_sum.shape, jnp.float32)
    spread_heads([(wide, query), (wide_grad, grad)], heads, head, block_rows)
    index = begin + lax.broadcasted_iota(jnp.int32, (1, block_rows), 1)
    for h in range(heads):
        rows = pl.ds(h * head, head)
        columns = pl.ds(h * block_rows, block_rows)
        first[:, columns] = start[...]
        last[:, columns] = index
        sums[:, columns] = logsum[pl.ds(h, 1), :]
        delta[:, columns] = jnp.sum(
            grad[rows, :].astype(jnp.float32) * out[rows, :], axis=0, keepdims=True
        )

    def body(block, masked):
        keys = pl.ds(pl.multiple_of(block * key_block, key_block), key_block)
        key_wide = pair[0, :head, keys]
        key = key_wide.T
        value = pair[0, head:, keys].T
        scores = dot(key, wide[...], 1, 0) * (scale * LOG2E)
        probs = jnp.exp2(scores - sums[...])
        if masked:
            allowed = allowed_pairs(block, key_block, first[...], last[...])
            probs = jnp.where(allowed, probs, 0.0)
        pair_sum[head:, keys] += dot(wide_grad[...], probs.astype(jnp.bfloat16), 1, 1)
        prob_grad = dot(value, wide_grad[...], 1, 0)
        score_grad = (probs * (prob_grad - delta[...])).astype(jnp.bfloat16)
        pair_sum[:head, keys] += dot(wide[...], score_grad, 1, 1)
        query_sum[...] += dot(key_wide, score_grad, 1, 0)

    over_blocks(plan, 4 * pl.program_id(0), body)
    half = ROT // 2
    for h in range(heads):
        value = query_sum[:, pl.ds(h * block_rows, block_rows)] * scale
        near, far = value[:half], value[half:ROT]
        turned = jnp.concatenate(
            [
                near * cosine[...] + far * sine[...],
                far * cosine[...] - near * sine[...],
                value[ROT:],
            ],
            axis=0,
        )
        query_grad[pl.ds(h * head, head), :] = turned.astype(jnp.bfloat16)

    @pl.when(pl.program_id(0) == pl.num_programs(0) - 1)
    def _():
        pair_grad[:head, :] = (pair_sum[:head, :] * scale).astype(jnp.bfloat16)
        pair_grad[head:, :] = pair_sum[head:, :].astype(jnp.bfloat16)


def attention_cost(micro, rows, length, products):
    pairs = micro * (rows // 64) * length * 2 * length
    return pl.CostEstimate(
        flops=2 * products * 64 * pairs, bytes_accessed=8 * micro * rows * length, transcendentals=pairs
    )


def attend_forward(start, query, pair, before, heads, head):
    micro, _, window = pair.shape
    rows, count = query.shape
    length = count // micro
    query_block, key_block = forward_blocks
    blocks = length // query_block
    spread = heads * query_block
    plan = block_plan(start, before, length, query_block, key_block).reshape(-1)
    column = lambda m, i, plan: (0, m * blocks + i)
    tall = pl.BlockSpec((rows, query_block), column)
    return pl.pallas_call(
        functools.partial(forward_kernel, before, heads, head, key_block),
        grid_spec=pltpu.PrefetchScalarGridSpec(
            num_scalar_prefetch=1,
            grid=(micro, blocks),
            in_specs=[
                tall,
                pl.BlockSpec((1, 2 * head, window), lambda m, i, plan: (m, 0, 0)),
                pl.BlockSpec((1, query_block), column),
            ],
            out_specs=[tall, tall, pl.BlockSpec((heads, query_block), column)],
            scratch_shapes=[
                pltpu.VMEM((head, spread), jnp.bfloat16),
                pltpu.VMEM((1, spread), jnp.float32),
                pltpu.VMEM((1, spread), jnp.float32),
                pltpu.VMEM((head, spread), jnp.float32),
                pltpu.VMEM((1, spread), jnp.int32),
                pltpu.VMEM((1, spread), jnp.int32),
            ],
        ),
        out_shape=[
            jax.ShapeDtypeStruct((rows, count), jnp.float32),
            jax.ShapeDtypeStruct((rows, count), jnp.bfloat16),
            jax.ShapeDtypeStruct((heads, count), jnp.float32),
        ],
        compiler_params=pltpu.CompilerParams(vmem_limit_bytes=40 << 20),
        cost_estimate=attention_cost(micro, rows, length, 2),
        name="attend_forward",
    )(plan, query, pair, start.reshape(1, count))


def attend_backward(at, start, query, pair, grad, out, logsum, cosine, sine, before, heads, head):
    micro, _, window = pair.shape
    rows, count = query.shape
    length = count // micro
    query_block, key_block = backward_blocks
    blocks = length // query_block
    spread = heads * query_block
    plan = block_plan(start, before, length, query_block, key_block)[at].reshape(-1)
    column = lambda i, plan: (0, at * blocks + i)
    tall = pl.BlockSpec((rows, query_block), column)
    table = pl.BlockSpec((ROT // 2, query_block), column)
    return pl.pallas_call(
        functools.partial(backward_kernel, before, heads, head, key_block),
        grid_spec=pltpu.PrefetchScalarGridSpec(
            num_scalar_prefetch=1,
            grid=(blocks,),
            in_specs=[
                tall,
                pl.BlockSpec((1, 2 * head, window), lambda i, plan: (at, 0, 0)),
                pl.BlockSpec((1, query_block), column),
                tall,
                tall,
                pl.BlockSpec((heads, query_block), column),
                table,
                table,
            ],
            out_specs=[
                pl.BlockSpec((rows, query_block), lambda i, plan: (0, i)),
                pl.BlockSpec((2 * head, window), lambda i, plan: (0, 0)),
            ],
            scratch_shapes=[
                pltpu.VMEM((head, spread), jnp.bfloat16),
                pltpu.VMEM((head, spread), jnp.bfloat16),
                pltpu.VMEM((head, spread), jnp.float32),
                pltpu.VMEM((2 * head, window), jnp.float32),
                pltpu.VMEM((1, spread), jnp.float32),
                pltpu.VMEM((1, spread), jnp.float32),
                pltpu.VMEM((1, spread), jnp.int32),
                pltpu.VMEM((1, spread), jnp.int32),
            ],
        ),
        out_shape=[
            jax.ShapeDtypeStruct((rows, length), jnp.bfloat16),
            jax.ShapeDtypeStruct((2 * head, window), jnp.bfloat16),
        ],
        compiler_params=pltpu.CompilerParams(vmem_limit_bytes=40 << 20),
        cost_estimate=attention_cost(1, rows, length, 5),
        name="attend_backward",
    )(plan, query, pair, start.reshape(1, count), grad, out, logsum, cosine, sine)


def shards(
    tokens,
    segments,
    query_weight,
    query_bias,
    key_weight,
    key_bias,
    value_weight,
    value_bias,
    output_weight,
    output_bias,
    upward_weight,
    upward_bias,
    down_weight,
    down_bias,
    attend_gain,
    attend_bias,
    dense_gain,
    dense_bias,
    cotangent,
):
    low = jnp.bfloat16
    micro, _, length, width = tokens.shape
    count = micro * length
    head = key_weight.shape[1]
    query_width = query_bias.shape[0]
    heads = query_width // head
    hidden_width = upward_bias.shape[0]
    devices = lax.axis_size("fsdp") * lax.axis_size("ctx")
    reach = lax.axis_size("ctx") // 2
    before = reach * length
    window = before + length
    core = lax.axis_index("tp")
    stages = all_bits()
    deep = [s for s in stages if s[0] == "ctx" and s[1] > 1]
    near = [s for s in stages if s[0] == "ctx" and s[1] == 1]
    side = [s for s in stages if s[0] == "fsdp"]

    first_half = core == 0

    def halves(own, other):
        return jnp.where(first_half, own, other), jnp.where(first_half, other, own)

    shard_rows = key_weight.shape[0]
    segment_piece = (segments + 1).astype(low).reshape(-1, head)
    piece_rows = max(shard_rows, segment_piece.shape[0])

    def padded(values):
        return jnp.pad(values, ((0, piece_rows - values.shape[0]), (0, 0)))

    pair_piece = jnp.concatenate(
        [padded(jnp.where(first_half, key_weight, value_weight)), padded(segment_piece)], axis=1
    )
    early = (pair_piece[None], [])
    asked = (query_weight[None], [])
    up = (upward_weight[None], [])
    down = (jnp.concatenate([down_weight.T, output_weight.T], axis=1)[None], [])
    up_order = deep + side + near
    down_order = deep + near + side
    for i, stage in enumerate(side + near + deep):
        early = gather_step(early, stage)
        if i < len(stages) - 2:
            up = gather_step(up, up_order[i])
            down = gather_step(down, down_order[i])
    for stage in near + side + deep:
        asked = gather_step(asked, stage)
    early_all = early[0]
    w_pair = early_all[:, :shard_rows, :head].reshape(width, head)
    w_query = asked[0].reshape(width, query_width)
    segment_all = early_all[:, : segment_piece.shape[0], head:].reshape(
        lax.axis_size("fsdp"), lax.axis_size("ctx"), micro, length
    )

    mine = lax.dynamic_index_in_dim(segment_all, lax.axis_index("fsdp"), 0, keepdims=False)
    reached = jnp.concatenate([jnp.zeros((reach,) + mine.shape[1:], low), mine])
    seen = lax.dynamic_slice_in_dim(reached, lax.axis_index("ctx"), reach + 1)
    seen = jnp.transpose(seen, (1, 0, 2)).reshape(micro, window).astype(jnp.int32)
    local = segments[:, 0] + 1
    start = jnp.sum((seen[:, None, :] < local[:, :, None]).astype(jnp.int32), axis=2)
    positions = (before + jnp.arange(length, dtype=jnp.int32))[None] - start
    freqs = jnp.exp(
        jnp.arange(ROT // 2, dtype=jnp.float32) * (-2.0 * math.log(10000.0) / ROT)
    )
    angle = freqs[:, None] * positions.reshape(1, count).astype(jnp.float32)
    cosine, sine = jnp.cos(angle), jnp.sin(angle)
    pair_cosine = jnp.where(first_half, cosine, 1.0)
    pair_sine = jnp.where(first_half, sine, 0.0)

    inputs = tokens.reshape(count, width).astype(jnp.float32)
    normed, spread = norm_parts(inputs)
    attend_in = (normed * attend_gain + attend_bias).astype(low)
    dense_in = (normed * dense_gain + dense_bias).astype(low)

    def by_micro(values):
        return jnp.transpose(values.reshape(head, micro, length), (1, 0, 2)).reshape(-1, length)

    def by_token(values):
        return jnp.transpose(values.reshape(micro, head, length), (1, 0, 2)).reshape(head, count)

    pair_lin = dot(w_pair, attend_in, 0, 1) + jnp.where(first_half, key_bias, value_bias)[:, None]
    pair_mine = by_micro(rotate(pair_lin, pair_cosine, pair_sine).astype(low))
    context = lax.axis_size("ctx")
    pair_mine = after(pair_mine, up[0], down[0])
    parts = [pair_mine]
    for d in range(1, reach + 1):
        parts.append(lax.ppermute(pair_mine, "ctx", [(i, i + d) for i in range(context - d)]))
    up = gather_step(up, up_order[-2])
    down = gather_step(down, down_order[-2])
    pair_half = jnp.concatenate(parts[::-1], axis=1)
    pair_other = partner(pair_half, ("tp", 1))
    pair = jnp.concatenate(
        [side_half.reshape(micro, head, window) for side_half in halves(pair_half, pair_other)],
        axis=1,
    )

    query_lin = dot(w_query, attend_in, 0, 1) + query_bias[:, None]
    query = (
        rotate(query_lin.reshape(heads, head, count), cosine, sine)
        .astype(low)
        .reshape(query_width, count)
    )
    query = after(query, up[0], down[0])
    attended, attended_low, logsum = attend_forward(start, query, pair, before, heads, head)
    w_upward = gather_step(up, up_order[-1])[0].reshape(width, hidden_width)
    w_down = gather_step(down, down_order[-1])[0].reshape(width, hidden_width + query_width)
    w_down, w_output = w_down[:, :hidden_width], w_down[:, hidden_width:]

    grad_low = cotangent.reshape(count, width)
    grad_full = grad_low.astype(jnp.float32)
    hidden_pre = dot(after(dense_in, attended_low), w_upward, 1, 0) + upward_bias
    normal_cdf = 0.5 * (1.0 + lax.erf(hidden_pre * (1.0 / math.sqrt(2.0))))
    normal_pdf = jnp.exp(-0.5 * hidden_pre * hidden_pre) * (1.0 / math.sqrt(2.0 * math.pi))
    hidden = (hidden_pre * normal_cdf).astype(low)
    slope = normal_cdf + hidden_pre * normal_pdf
    pre_grad = (dot(grad_low, w_down, 1, 0) * slope).astype(low)

    def by_device(values):
        return values.astype(low).reshape(devices, shard_rows, values.shape[1])

    up_order = side + near + deep[::-1]
    down_order = near + side + deep[::-1]
    up = (by_device(dot(dense_in, pre_grad, 0, 0)), stages)
    down = jnp.concatenate(
        [dot(grad_low, hidden, 0, 0).astype(low), dot(grad_low, attended_low, 0, 1).astype(low)],
        axis=1,
    )
    down = (by_device(down), stages)
    up = scatter_step(up, up_order[0])
    down = scatter_step(down, down_order[0])

    attended_grad = dot(w_output, grad_low, 0, 1).astype(low)
    query_grads, pair_grads = [], []
    for at in range(micro):
        if at == micro - 1:
            attended_grad = after(attended_grad, up[0], down[0])
            up = scatter_step(up, up_order[1])
            down = scatter_step(down, down_order[1])
        query_part, pair_part = attend_backward(
            at, start, query, pair, attended_grad, attended, logsum, cosine, sine, before, heads, head
        )
        query_grads.append(query_part)
        pair_grads.append(pair_part)
    query_grad = jnp.concatenate(query_grads, axis=1)
    pair_back = jnp.stack(pair_grads).reshape(micro, 2, head, window)

    keep, send = halves(pair_back[:, 0], pair_back[:, 1])
    summed = (keep.astype(jnp.float32) + partner(send, ("tp", 1)).astype(jnp.float32)).astype(low)
    summed = summed.reshape(micro * head, window)
    pair_sum = summed[:, before:].astype(jnp.float32)
    for d in range(1, reach + 1):
        piece = summed[:, before - d * length : before - (d - 1) * length]
        pair_sum = pair_sum + lax.ppermute(
            piece, "ctx", [(i + d, i) for i in range(context - d)]
        ).astype(jnp.float32)
    pair_low = rotate(by_token(pair_sum), pair_cosine, -pair_sine).astype(low)

    asked_order = side + near + deep[::-1]
    asked = (by_device(dot(attend_in, query_grad, 0, 1)), stages)
    for stage in asked_order:
        asked = scatter_step(asked, stage)
    for up_stage, down_stage in zip(up_order[2:], down_order[2:]):
        up = scatter_step(up, up_stage)
        down = scatter_step(down, down_stage)
    grad_query, grad_up, grad_down = asked[0][0], up[0][0], down[0][0]

    dense_part = dot(pre_grad, w_upward, 1, 1)
    attend_part = dot(query_grad, w_query, 0, 1) + dot(pair_low, w_pair, 0, 1)
    norm_part = (attend_part * attend_gain + dense_part * dense_gain).astype(low)
    norm_grad = norm_part.astype(jnp.float32) + partner(norm_part, ("tp", 1)).astype(jnp.float32)
    tokens_grad = (
        grad_full
        + spread
        * (
            norm_grad
            - jnp.mean(norm_grad, axis=-1, keepdims=True)
            - normed * jnp.mean(norm_grad * normed, axis=-1, keepdims=True)
        )
    ).astype(low)

    branches = (dot(attended_low, w_output, 0, 1) + dot(hidden, w_down, 1, 1)).astype(low)
    mixed = branches.astype(jnp.float32) + partner(branches, ("tp", 1)).astype(jnp.float32)
    result = (inputs + mixed + output_bias + down_bias).astype(low)

    small = jnp.concatenate(
        [
            jnp.sum(attend_part * normed, axis=0),
            jnp.sum(attend_part, axis=0),
            jnp.sum(dense_part * normed, axis=0),
            jnp.sum(dense_part, axis=0),
            jnp.pad(jnp.sum(pair_low.astype(jnp.float32), axis=1), (0, -head % LANES)),
            jnp.sum(grad_full, axis=0),
            jnp.sum(pre_grad.astype(jnp.float32), axis=0),
            jnp.sum(query_grad.astype(jnp.float32), axis=1),
        ]
    ).reshape(-1, LANES)
    shared_rows = 4 * width // LANES + 1
    piece_rows = shard_rows * head // LANES
    held = dot(attend_in, pair_low, 0, 1).reshape(devices, piece_rows, LANES)
    left = stages
    for stage in asked_order:
        send, keep = scatter_halves(held, left, stage)
        left = [other for other in left if other != stage]
        rows = send.shape[0] * piece_rows
        got = partner(jnp.concatenate([send.reshape(rows, LANES), small]), stage)
        held = keep + got[:rows].reshape(keep.shape)
        small = small + got[rows:]
    own = jnp.concatenate([held[0], small[:shared_rows]])
    got = partner(own, ("tp", 1))
    grad_key, grad_value = [
        values.reshape(shard_rows, head) for values in halves(held[0], got[:piece_rows])
    ]
    shared = small[: shared_rows - 1] + got[piece_rows : piece_rows + shared_rows - 1]
    g_gain, g_shift, d_gain, d_shift = jnp.split(shared.reshape(-1), 4)
    k_b, v_b = [values[:head] for values in halves(small[shared_rows - 1], got[-1])]
    rest = small[shared_rows:].reshape(-1)
    out_b, up_b, q_b = jnp.split(rest, [width, width + hidden_width])
    shape = (micro, 1, length, width)
    return (
        result.reshape(shape),
        tokens_grad.reshape(shape),
        grad_query,
        q_b,
        grad_key,
        k_b,
        grad_value,
        v_b,
        grad_down[:, hidden_width:].T,
        out_b,
        grad_up,
        up_b,
        grad_down[:, :hidden_width].T,
        out_b,
        g_gain,
        g_shift,
        d_gain,
        d_shift,
    )


def solution(mesh):
    return jax.shard_map(
        shards,
        mesh=mesh,
        in_specs=(
            P(None, "fsdp", "ctx", None),
            P(None, "fsdp", "ctx"),
            P(("fsdp", "ctx"), "tp"),
            P("tp"),
            P(("fsdp", "ctx"), None),
            P(),
            P(("fsdp", "ctx"), None),
            P(),
            P("tp", ("fsdp", "ctx")),
            P(),
            P(("fsdp", "ctx"), "tp"),
            P("tp"),
            P("tp", ("fsdp", "ctx")),
            P(),
            P(),
            P(),
            P(),
            P(),
            P(None, "fsdp", "ctx", None),
        ),
        out_specs=(
            P(None, "fsdp", "ctx", None),
            P(None, "fsdp", "ctx", None),
            P(("fsdp", "ctx"), "tp"),
            P("tp"),
            P(("fsdp", "ctx"), None),
            P(),
            P(("fsdp", "ctx"), None),
            P(),
            P("tp", ("fsdp", "ctx")),
            P(),
            P(("fsdp", "ctx"), "tp"),
            P("tp"),
            P("tp", ("fsdp", "ctx")),
            P(),
            P(),
            P(),
            P(),
            P(),
        ),
        check_vma=False,
    )
```

time: 370 us -> 293 us (0.79)
  waiting for transfers between devices: 133 us -> 83.7 us
  starting transfers between devices: 120 us -> 83.6 us
  other arithmetic: 29.2 us -> 42.1 us
  between operations: 15.3 us -> 2.75 us
  local copies, waits for them, and re-layouts: 15 us -> 23 us
  Pallas kernels: 24.6 us -> 18.8 us
  matrix products: 31.8 us -> 35.9 us
    all_gather x1 -> x0, waiting for transfers between devices: 49.4 us -> none  [shards(): lax.all_gather(jnp.concatenate([query_weight, output_weight.T, upward_wei...]
    ppermute x30 -> x37, starting transfers between devices: 102 us -> 66.2 us  [partner(): return lax.ppermute(values, name, pairs)]
    select_n x23 -> x38, other arithmetic: 4.32 us -> 13.7 us  [the longest x16 7.83 us: gather_step(): jnp.where(upper, other, split)]
    ppermute x30 -> x37, waiting for transfers between devices: 68.7 us -> 75.1 us  [partner(): return lax.ppermute(values, name, pairs)]
    concatenate x4 -> x9, local copies, waits for them, and re-layouts: 0.04 us -> 6.06 us  [the longest x1 4.67 us: shards(): jnp.concatenate([dot(grad_low, hidden, 0, 0).astype(low), dot(grad_low, a...]
    pallas_call x2 -> x3, Pallas kernels: 24.6 us -> 18.8 us  [the longest x2 10.8 us: attend_backward(): pl.pallas_call(functools.partial(backward_kernel, before, heads, head, ke...]
    dot_general x15, matrix products: 31.8 us -> 35.9 us  [dot(): lax.dot_general(left, right, (((left_dim,), (right_dim,)), ((), ())), pre...]
    unnamed x87 -> x113, local copies, waits for them, and re-layouts: 6.96 us -> 7.59 us
  transfers between devices with their start and end apart: 39 -> 45, of which waited for: 26 -> 20; matrix products, arithmetic and copies ran while one was open for 16% -> 30% of each run, Pallas kernels for 7% -> 6%
where the time goes in v2:
time: 293 us; the launch traced here: 290 us
  waiting for transfers between devices  83.7 us (29%)
  starting transfers between devices  83.6 us (29%)
  other arithmetic  42.1 us (14%)
  matrix products  35.9 us (12%)
  local copies, waits for them, and re-layouts  23 us (8%)
  Pallas kernels  18.8 us (6%)
    ppermute x37, waiting for transfers between devices, partner(): return lax.ppermute(values, name, pairs)  75.1 us
    ppermute x37, starting transfers between devices, partner(): return lax.ppermute(values, name, pairs)  66.2 us
    dot_general x15, matrix products, dot(): lax.dot_general(left, right, (((left_dim,), (right_dim,)), ((), ())), pre...  35.9 us
    ppermute x4, starting transfers between devices, shards(): lax.ppermute(pair_mine, 'ctx', [(i, i + d) for i in range(context - d)])  12 us
    pallas_call x2, Pallas kernels, attend_backward(): pl.pallas_call(functools.partial(backward_kernel, before, heads, head, ke...  10.8 us
    pallas_call x1, Pallas kernels, attend_forward(): pl.pallas_call(functools.partial(forward_kernel, before, heads, head, key...  8.03 us
    select_n x16, other arithmetic, gather_step(): jnp.where(upper, other, split)  7.83 us
    unnamed x113, local copies, waits for them, and re-layouts  7.59 us
  transfers between devices with their start and end apart: 45, of which 20 were waited for; matrix products, arithmetic and copies ran while one was open for 30% of the time, Pallas kernels for 6%

profile of v2, /device:TPU:0, one launch (start us, length us, event | category | flops | bytes accessed | tf_op | source)
XLA Modules:
  0.0 290.0 jit_solution(10097882312120614634)
XLA Ops:
  0.7 4.1 %collective-permute-start.8 = (bf16[1,48,1536]{2,1,0:T(8,128)(2,1)}, bf16[1,48,1536]{2,1,0:T(8,128)(2,1)}, u32[]{:S(2)}, u32[]{:S(2)}) collective-permute-start(bf16[1,48,1536]{2,1,0:T(8,128)(2,1)} %bitcast.638), channel_id=1, source_target_pairs={{0,8},{2,10},{4,12},{6,14},{8,0},{10,2},{12,4},{14,6},{1,9},{3,11}... | collective-permute-start | bytes 442376 | tf_op jit(solution)/shard_map/ppermute | solution.py:40
  45.5 5.6 %collective-permute-done.12 = bf16[2,48,1920]{2,1,0:T(8,128)(2,1)} collective-permute-done((bf16[2,48,1920]{2,1,0:T(8,128)(2,1)}, bf16[2,48,1920]{2,1,0:T(8,128)(2,1)}, u32[]{:S(2)}, u32[]{:S(2)}) %collective-permute-start.12) | collective-permute-done | bytes 368672 | tf_op jit(solution)/shard_map/ppermute | solution.py:40
  52.3 3.5 %collective-permute-start.14 = (bf16[128,512]{1,0:T(8,128)(2,1)S(1)}, bf16[128,512]{1,0:T(8,128)(2,1)S(1)}, u32[]{:S(2)}, u32[]{:S(2)}) collective-permute-start(bf16[128,512]{1,0:T(8,128)(2,1)S(1)} %bitcast.617), channel_id=1, source_target_pairs={{0,8},{2,10},{4,12},{6,14},{1,9},{3,11},{5,13},{7,15},{16,24},{18,... | collective-permute-start | bytes 393224 | tf_op jit(solution)/shard_map/ppermute | solution.py:458
  55.8 3.8 %collective-permute-start.15 = (bf16[128,512]{1,0:T(8,128)(2,1)S(1)}, bf16[128,512]{1,0:T(8,128)(2,1)S(1)}, u32[]{:S(2)}, u32[]{:S(2)}) collective-permute-start(bf16[128,512]{1,0:T(8,128)(2,1)S(1)} %bitcast.618), channel_id=1, source_target_pairs={{0,6},{2,8},{4,10},{6,12},{8,14},{1,7},{3,9},{5,11},{7,13},{9,15},... | collective-permute-start | bytes 393224 | tf_op jit(solution)/shard_map/ppermute | solution.py:458
  61.0 3.4 %collective-permute-start.17 = (bf16[128,512]{1,0:T(8,128)(2,1)S(1)}, bf16[128,512]{1,0:T(8,128)(2,1)S(1)}, u32[]{:S(2)}, u32[]{:S(2)}) collective-permute-start(bf16[128,512]{1,0:T(8,128)(2,1)S(1)} %bitcast.620), channel_id=1, source_target_pairs={{0,2},{2,4},{4,6},{6,8},{8,10},{10,12},{12,14},{1,3},{3,5},{5,7},{... | collective-permute-start | bytes 393224 | tf_op jit(solution)/shard_map/ppermute | solution.py:458
  71.2 10.9 %collective-permute-done.13 = bf16[4,48,1920]{2,1,0:T(8,128)(2,1)S(1)} collective-permute-done((bf16[4,48,1920]{2,1,0:T(8,128)(2,1)S(1)}, bf16[4,48,1920]{2,1,0:T(8,128)(2,1)S(1)}, u32[]{:S(2)}, u32[]{:S(2)}) %collective-permute-start.13) | collective-permute-done | bytes 737312 | tf_op jit(solution)/shard_map/ppermute | solution.py:40
  84.4 8.0 %attend_forward.1 = (f32[384,1024]{1,0:T(8,128)S(1)}, bf16[384,1024]{1,0:T(8,128)(2,1)S(1)}, f32[6,1024]{1,0:T(8,128)S(1)}) custom-call(s32[8]{0:T(128)S(1)} %reshape.1428.plan, bf16[384,1024]{1,0:T(8,128)(2,1)S(1)} %bitcast.550, bf16[2,128,2560]{2,1,0:T(8,128)(2,1)S(1)} %pad_maximum_fusion.4.pair, s32[1,1024]{1,0:T(1,128)S(1)} %bitcast.553), custom_call_target="tpu_custom_call" | custom-call | flops 1610612736 | bytes 3145728 | tf_op jit(solution)/shard_map/attend_forward/pallas_call | solution.py:271
  93.6 9.0 %collective-permute-done.20 = bf16[8,48,1536]{2,1,0:T(8,128)(2,1)S(1)} collective-permute-done((bf16[8,48,1536]{2,1,0:T(8,128)(2,1)S(1)}, bf16[8,48,1536]{2,1,0:T(8,128)(2,1)S(1)}, u32[]{:S(2)}, u32[]{:S(2)}) %collective-permute-start.20) | collective-permute-done | bytes 1179680 | tf_op jit(solution)/shard_map/ppermute | solution.py:40
  104.8 5.0 %multiply_convert_fusion = (bf16[1024,1536]{1,0:T(8,128)(2,1)S(1)}, f32[1024,1536]{1,0:T(8,128)}) fusion(f32[1536]{0:T(1024)S(1)} %copy-done.36, bf16[1024,768]{1,0:T(8,128)(2,1)S(1)} %copy-done.16, bf16[768,1536]{1,0:T(8,128)(2,1)S(1)} %bitcast.591), kind=kOutput, calls=%fused_computation.9 | convolution fusion | flops 2425356288 | bytes 13375488 | tf_op jit(solution)/shard_map/dot_general | solution.py:21
  114.5 4.7 %copy.252 = bf16[768,1920]{1,0:T(8,128)(2,1)} copy(bf16[768,1920]{0,1:T(8,128)(2,1)} %pad_maximum_fusion.1) | data formatting | bytes 5898240 | tf_op jit(solution)/shard_map/concatenate | solution.py:495
  126.8 5.6 %convert_reduce_fusion.1 = (f32[1536]{0:T(1024)S(1)}, bf16[1024,1536]{1,0:T(8,128)(2,1)S(1)}) fusion(f32[1024,1536]{1,0:T(8,128)S(1)} %bitcast.671, f32[1536]{0:T(1024)S(1)} %copy-done.36, bf16[1024,768]{1,0:T(8,128)(2,1)S(1)} %bitcast.570, bf16[768,1920]{1,0:T(8,128)(2,1)S(1)} %bitcast.575), kind=kOutput, calls=%fused_computation.8 | convolution fusion | flops 2436364800 | bytes 13383680 | tf_op jit(solution)/shard_map/dot_general | solution.py:21
  137.6 3.7 %add_convert_fusion.1 = bf16[1024,768]{1,0:T(8,128)(2,1)} fusion(f32[1024,768]{1,0:T(8,128)S(1)} %fusion.55, bf16[1024,1536]{1,0:T(8,128)(2,1)S(1)} %copy-done.43, bf16[768,1920]{1,0:T(8,128)(2,1)S(1)} %bitcast.577), kind=kOutput, calls=%fused_computation.47 | convolution fusion | flops 2417491968 | bytes 10223616 | tf_op jit(solution)/shard_map/dot_general | solution.py:21
  142.7 5.4 %attend_backward.2 = (bf16[384,512]{1,0:T(8,128)(2,1)S(1)}, bf16[128,2560]{1,0:T(8,128)(2,1)S(1)}) custom-call(s32[8]{0:T(128)S(1)} %reshape_squeeze.6.plan, bf16[384,1024]{1,0:T(8,128)(2,1)S(1)} %bitcast.551, bf16[2,128,2560]{2,1,0:T(8,128)(2,1)S(1)} %pad_maximum_fusion.4.pair, s32[1,1024]{1,0:T(1,128)S(1)} %bitcast.554, ...), custom_call_target="tpu_custom_call" | custom-call | flops 2013265920 | bytes 1572864 | tf_op jit(solution)/shard_map/attend_backward/pallas_call | solution.py:313
  152.3 13.4 %collective-permute-done.22 = bf16[8,48,1536]{2,1,0:T(8,128)(2,1)S(1)} collective-permute-done((bf16[8,48,1536]{2,1,0:T(8,128)(2,1)S(1)}, bf16[8,48,1536]{2,1,0:T(8,128)(2,1)S(1)}, u32[]{:S(2)}, u32[]{:S(2)}) %collective-permute-start.22) | collective-permute-done | bytes 1179680 | tf_op jit(solution)/shard_map/ppermute | solution.py:40
  166.6 5.4 %attend_backward.3 = (bf16[384,512]{1,0:T(8,128)(2,1)S(1)}, bf16[128,2560]{1,0:T(8,128)(2,1)S(1)}) custom-call(s32[8]{0:T(128)S(1)} %reshape_squeeze.7.plan, bf16[384,1024]{1,0:T(8,128)(2,1)S(1)} %bitcast.552, bf16[2,128,2560]{2,1,0:T(8,128)(2,1)S(1)} %pad_maximum_fusion.4.pair, s32[1,1024]{1,0:T(1,128)S(1)} %bitcast.555, ...), custom_call_target="tpu_custom_call" | custom-call | flops 2013265920 | bytes 1572864 | tf_op jit(solution)/shard_map/attend_backward/pallas_call | solution.py:313
  184.6 5.5 %collective-permute-start.40 = (bf16[2,48,1920]{2,1,0:T(8,128)(2,1)}, bf16[2,48,1920]{2,1,0:T(8,128)(2,1)}, u32[]{:S(2)}, u32[]{:S(2)}) collective-permute-start(bf16[2,48,1920]{2,1,0:T(8,128)(2,1)} %select_bitcast_fusion.11), channel_id=1, source_target_pairs={{0,4},{2,6},{4,0},{6,2},{8,12},{10,14},{12,8},{14,10},{1,5},{3,7},... | collective-permute-start | bytes 1105928 | tf_op jit(solution)/shard_map/ppermute | solution.py:40
  190.2 29.5 %collective-permute-start.43 = (bf16[2,48,1536]{2,1,0:T(8,128)(2,1)}, bf16[2,48,1536]{2,1,0:T(8,128)(2,1)}, u32[]{:S(2)}, u32[]{:S(2)}) collective-permute-start(bf16[2,48,1536]{2,1,0:T(8,128)(2,1)} %fusion.59), channel_id=1, source_target_pairs={{0,4},{2,6},{4,0},{6,2},{8,12},{10,14},{12,8},{14,10},{1,5},{3,7},... | collective-permute-start | bytes 884744 | tf_op jit(solution)/shard_map/ppermute | solution.py:40
  219.7 5.3 %collective-permute-done.28 = bf16[128,512]{1,0:T(8,128)(2,1)S(1)} collective-permute-done((bf16[128,512]{1,0:T(8,128)(2,1)S(1)}, bf16[128,512]{1,0:T(8,128)(2,1)S(1)}, u32[]{:S(2)}, u32[]{:S(2)}) %collective-permute-start.28) | collective-permute-done | bytes 131104 | tf_op jit(solution)/shard_map/ppermute | solution.py:524
  229.8 7.5 %fusion.84 = (f32[768]{0:T(1024)S(1)}, f32[768]{0:T(1024)}, bf16[1024,768]{1,0:T(8,128)(2,1)}, f32[768]{0:T(1024)}, f32[768]{0:T(1024)}, /*index=5*/bf16[1024,768]{1,0:T(8,128)(2,1)S(1)}, bf16[1024,768]{1,0:T(8,128)(2,1)}) fusion(f32[1024]{0:T(1024)S(1)} %bitcast.646, f32[1024]{0:T(1024)S(1)} %bitcast.650, bf16[2,1,512,768]{3,2,1,0:T(8,128)(2,1)S(1)} %copy-done.3, ...), kind=kOutput, calls=%fused_computation.314 | convolution fusion | flops 2434003968 | bytes 18123776 | tf_op jit(solution)/shard_map/dot_general | solution.py:21
  254.6 3.9 %collective-permute-done.36 = f32[94,128]{1,0:T(8,128)S(1)} collective-permute-done((f32[94,128]{1,0:T(8,128)S(1)}, f32[94,128]{1,0:T(8,128)S(1)}, u32[]{:S(2)}, u32[]{:S(2)}) %collective-permute-start.36) | collective-permute-done | bytes 48160 | tf_op jit(solution)/shard_map/ppermute | solution.py:40
  260.0 3.3 %collective-permute-done.44 = bf16[1,48,1536]{2,1,0:T(8,128)(2,1)S(1)} collective-permute-done((bf16[1,48,1536]{2,1,0:T(8,128)(2,1)S(1)}, bf16[1,48,1536]{2,1,0:T(8,128)(2,1)S(1)}, u32[]{:S(2)}, u32[]{:S(2)}) %collective-permute-start.44) | collective-permute-done | bytes 147488 | tf_op jit(solution)/shard_map/ppermute | solution.py:40
  267.3 5.2 %collective-permute-done.31 = bf16[4,48,384]{2,1,0:T(8,128)(2,1)S(1)} collective-permute-done((bf16[4,48,384]{2,1,0:T(8,128)(2,1)S(1)}, bf16[4,48,384]{2,1,0:T(8,128)(2,1)S(1)}, u32[]{:S(2)}, u32[]{:S(2)}) %collective-permute-start.31) | collective-permute-done | bytes 147488 | tf_op jit(solution)/shard_map/ppermute | solution.py:40
  273.2 3.8 %collective-permute-done.32 = bf16[2,48,384]{2,1,0:T(8,128)(2,1)S(1)} collective-permute-done((bf16[2,48,384]{2,1,0:T(8,128)(2,1)S(1)}, bf16[2,48,384]{2,1,0:T(8,128)(2,1)S(1)}, u32[]{:S(2)}, u32[]{:S(2)}) %collective-permute-start.32) | collective-permute-done | bytes 73760 | tf_op jit(solution)/shard_map/ppermute | solution.py:40
  285.4 3.5 %fusion.25 = bf16[1024,768]{1,0:T(8,128)(2,1)} fusion(bf16[2,1,512,768]{3,2,1,0:T(8,128)(2,1)S(1)} %copy-done.3, bf16[1024,768]{1,0:T(8,128)(2,1)} %collective-permute-done.29, bf16[1024,768]{1,0:T(8,128)(2,1)S(1)} %copy-done.9, f32[1024]{0:T(1024)S(1)} %broadcast_multiply_fusion, f32[1024]{0:T(1024)S(1)} %broadcast_multiply_fusion.1, ...), kind=kLoop, calls=%fused_computation.36 | loop fusion | flops 10223616 | bytes 7880704 | tf_op jit(solution)/shard_map/convert_element_type | solution.py:550
  (359 shorter events, 128.2 us)
Async XLA Ops:
  0.7 31.2 %collective-permute-start.8 = (bf16[1,48,1536]{2,1,0:T(8,128)(2,1)}, bf16[1,48,1536]{2,1,0:T(8,128)(2,1)}, u32[]{:S(2)}, u32[]{:S(2)}) collective-permute-start(bf16[1,48,1536]{2,1,0:T(8,128)(2,1)} %bitcast.638), channel_id=1, source_target_pairs={{0,8},{2,10},{4,12},{6,14},{8,0},{10,2},{12,4},{14,6},{1,9},{3,11}... | collective-permute-start | bytes 442376 | tf_op jit(solution)/shard_map/ppermute | solution.py:40
  6.4 29.6 %collective-permute-start.11 = (bf16[1,48,1920]{2,1,0:T(8,128)(2,1)}, bf16[1,48,1920]{2,1,0:T(8,128)(2,1)}, u32[]{:S(2)}, u32[]{:S(2)}) collective-permute-start(bf16[1,48,1920]{2,1,0:T(8,128)(2,1)} %maximum_bitcast_fusion.2), channel_id=1, source_target_pairs={{0,8},{2,10},{4,12},{6,14},{8,0},{10,2},{12,4},{14,6},{1,9},{3,11}... | collective-permute-start | bytes 552968 | tf_op jit(solution)/shard_map/ppermute | solution.py:40
  10.0 14.5 %collective-permute-start.4 = (bf16[1,48,384]{2,1,0:T(8,128)(2,1)}, bf16[1,48,384]{2,1,0:T(8,128)(2,1)S(1)}, u32[]{:S(2)}, u32[]{:S(2)}) collective-permute-start(bf16[1,48,384]{2,1,0:T(8,128)(2,1)} %bitcast.659), channel_id=1, source_target_pairs={{0,2},{2,0},{4,6},{6,4},{8,10},{10,8},{12,14},{14,12},{1,3},{3,1},... | collective-permute-start | bytes 110600 | tf_op jit(solution)/shard_map/ppermute | solution.py:40
  29.0 12.2 %collective-permute-start.6 = (bf16[4,48,384]{2,1,0:T(8,128)(2,1)S(1)}, bf16[4,48,384]{2,1,0:T(8,128)(2,1)}, u32[]{:S(2)}, u32[]{:S(2)}) collective-permute-start(bf16[4,48,384]{2,1,0:T(8,128)(2,1)S(1)} %bitcast.637), channel_id=1, source_target_pairs={{0,8},{2,10},{4,12},{6,14},{8,0},{10,2},{12,4},{14,6},{1,9},{3,11}... | collective-permute-start | bytes 442376 | tf_op jit(solution)/shard_map/ppermute | solution.py:40
  37.8 13.3 %collective-permute-start.12 = (bf16[2,48,1920]{2,1,0:T(8,128)(2,1)}, bf16[2,48,1920]{2,1,0:T(8,128)(2,1)}, u32[]{:S(2)}, u32[]{:S(2)}) collective-permute-start(bf16[2,48,1920]{2,1,0:T(8,128)(2,1)} %maximum_bitcast_fusion), channel_id=1, source_target_pairs={{0,4},{2,6},{4,0},{6,2},{8,12},{10,14},{12,8},{14,10},{1,5},{3,7},... | collective-permute-start | bytes 1105928 | tf_op jit(solution)/shard_map/ppermute | solution.py:40
  42.2 18.8 %collective-permute-start.7 = (bf16[8,48,384]{2,1,0:T(8,128)(2,1)S(1)}, bf16[8,48,384]{2,1,0:T(8,128)(2,1)S(1)}, u32[]{:S(2)}, u32[]{:S(2)}) collective-permute-start(bf16[8,48,384]{2,1,0:T(8,128)(2,1)S(1)} %bitcast.606), channel_id=1, source_target_pairs={{0,4},{2,6},{4,0},{6,2},{8,12},{10,14},{12,8},{14,10},{1,5},{3,7},... | collective-permute-start | bytes 884744 | tf_op jit(solution)/shard_map/ppermute | solution.py:40
  44.9 23.5 %collective-permute-start.10 = (bf16[4,48,1536]{2,1,0:T(8,128)(2,1)S(1)}, bf16[4,48,1536]{2,1,0:T(8,128)(2,1)S(1)}, u32[]{:S(2)}, u32[]{:S(2)}) collective-permute-start(bf16[4,48,1536]{2,1,0:T(8,128)(2,1)S(1)} %bitcast.590), channel_id=1, source_target_pairs={{0,16},{16,0},{1,17},{17,1},{2,18},{18,2},{3,19},{19,3},{4,20},{20... | collective-permute-start | bytes 1769480 | tf_op jit(solution)/shard_map/ppermute | solution.py:40
  52.3 13.4 %collective-permute-start.14 = (bf16[128,512]{1,0:T(8,128)(2,1)S(1)}, bf16[128,512]{1,0:T(8,128)(2,1)S(1)}, u32[]{:S(2)}, u32[]{:S(2)}) collective-permute-start(bf16[128,512]{1,0:T(8,128)(2,1)S(1)} %bitcast.617), channel_id=1, source_target_pairs={{0,8},{2,10},{4,12},{6,14},{1,9},{3,11},{5,13},{7,15},{16,24},{18,... | collective-permute-start | bytes 393224 | tf_op jit(solution)/shard_map/ppermute | solution.py:458
  65.7 16.4 %collective-permute-start.13 = (bf16[4,48,1920]{2,1,0:T(8,128)(2,1)S(1)}, bf16[4,48,1920]{2,1,0:T(8,128)(2,1)S(1)}, u32[]{:S(2)}, u32[]{:S(2)}) collective-permute-start(bf16[4,48,1920]{2,1,0:T(8,128)(2,1)S(1)} %bitcast.579), channel_id=1, source_target_pairs={{0,2},{2,0},{4,6},{6,4},{8,10},{10,8},{12,14},{14,12},{1,3},{3,1},... | collective-permute-start | bytes 2211848 | tf_op jit(solution)/shard_map/ppermute | solution.py:40
  68.3 15.9 %collective-permute-start.18 = (bf16[128,2560]{1,0:T(8,128)(2,1)S(1)}, bf16[128,2560]{1,0:T(8,128)(2,1)S(1)}, u32[]{:S(2)}, u32[]{:S(2)}) collective-permute-start(bf16[128,2560]{1,0:T(8,128)(2,1)S(1)} %constant_dynamic-update-slice_fusion), channel_id=1, source_target_pairs={{0,1},{1,0},{2,3},{3,2},{4,5},{5,4},{6,7},{7,6},{8,9},{9,8},{10,11... | collective-permute-start | bytes 1966088 | tf_op jit(solution)/shard_map/ppermute | solution.py:40
  68.6 34.0 %collective-permute-start.20 = (bf16[8,48,1536]{2,1,0:T(8,128)(2,1)S(1)}, bf16[8,48,1536]{2,1,0:T(8,128)(2,1)S(1)}, u32[]{:S(2)}, u32[]{:S(2)}) collective-permute-start(bf16[8,48,1536]{2,1,0:T(8,128)(2,1)S(1)} %bitcast.574), channel_id=1, source_target_pairs={{0,2},{2,0},{4,6},{6,4},{8,10},{10,8},{12,14},{14,12},{1,3},{3,1},... | collective-permute-start | bytes 3538952 | tf_op jit(solution)/shard_map/ppermute | solution.py:40
  83.6 39.7 %collective-permute-start.19 = (bf16[8,48,1920]{2,1,0:T(8,128)(2,1)}, bf16[8,48,1920]{2,1,0:T(8,128)(2,1)}, u32[]{:S(2)}, u32[]{:S(2)}) collective-permute-start(bf16[8,48,1920]{2,1,0:T(8,128)(2,1)} %bitcast.63), channel_id=1, source_target_pairs={{0,16},{16,0},{1,17},{17,1},{2,18},{18,2},{3,19},{19,3},{4,20},{20... | collective-permute-start | bytes 4423688 | tf_op jit(solution)/shard_map/ppermute | solution.py:40
  121.3 29.7 %collective-permute-start.23 = (bf16[8,48,1920]{2,1,0:T(8,128)(2,1)S(1)}, bf16[8,48,1920]{2,1,0:T(8,128)(2,1)S(1)}, u32[]{:S(2)}, u32[]{:S(2)}) collective-permute-start(bf16[8,48,1920]{2,1,0:T(8,128)(2,1)S(1)} %select_bitcast_fusion), channel_id=1, source_target_pairs={{0,2},{2,0},{4,6},{6,4},{8,10},{10,8},{12,14},{14,12},{1,3},{3,1},... | collective-permute-start | bytes 4423688 | tf_op jit(solution)/shard_map/ppermute | solution.py:40
  136.7 29.0 %collective-permute-start.22 = (bf16[8,48,1536]{2,1,0:T(8,128)(2,1)S(1)}, bf16[8,48,1536]{2,1,0:T(8,128)(2,1)S(1)}, u32[]{:S(2)}, u32[]{:S(2)}) collective-permute-start(bf16[8,48,1536]{2,1,0:T(8,128)(2,1)S(1)} %select_bitcast_fusion.3), channel_id=1, source_target_pairs={{0,16},{16,0},{1,17},{17,1},{2,18},{18,2},{3,19},{19,3},{4,20},{20... | collective-permute-start | bytes 3538952 | tf_op jit(solution)/shard_map/ppermute | solution.py:40
  141.3 86.4 %collective-permute-start.21 = (bf16[1024,768]{1,0:T(8,128)(2,1)}, bf16[1024,768]{1,0:T(8,128)(2,1)}, u32[]{:S(2)}, u32[]{:S(2)}) collective-permute-start(bf16[1024,768]{1,0:T(8,128)(2,1)} %add_convert_fusion.1), channel_id=1, source_target_pairs={{0,1},{1,0},{2,3},{3,2},{4,5},{5,4},{6,7},{7,6},{8,9},{9,8},{10,11... | collective-permute-start | bytes 4718600 | tf_op jit(solution)/shard_map/ppermute | solution.py:40
  151.7 23.8 %collective-permute-start.39 = (bf16[4,48,1920]{2,1,0:T(8,128)(2,1)S(1)}, bf16[4,48,1920]{2,1,0:T(8,128)(2,1)S(1)}, u32[]{:S(2)}, u32[]{:S(2)}) collective-permute-start(bf16[4,48,1920]{2,1,0:T(8,128)(2,1)S(1)} %select_bitcast_fusion.6), channel_id=1, source_target_pairs={{0,16},{16,0},{1,17},{17,1},{2,18},{18,2},{3,19},{19,3},{4,20},{20... | collective-permute-start | bytes 2211848 | tf_op jit(solution)/shard_map/ppermute | solution.py:40
  178.4 11.7 %collective-permute-start.26 = (bf16[128,512]{1,0:T(8,128)(2,1)S(1)}, bf16[128,512]{1,0:T(8,128)(2,1)S(1)}, u32[]{:S(2)}, u32[]{:S(2)}) collective-permute-start(bf16[128,512]{1,0:T(8,128)(2,1)S(1)} %get-tuple-element.165), channel_id=1, source_target_pairs={{4,0},{6,2},{8,4},{10,6},{12,8},{14,10},{5,1},{7,3},{9,5},{11,7},{... | collective-permute-start | bytes 393224 | tf_op jit(solution)/shard_map/ppermute | solution.py:524
  179.7 40.0 %collective-permute-start.27 = (bf16[128,512]{1,0:T(8,128)(2,1)S(1)}, bf16[128,512]{1,0:T(8,128)(2,1)S(1)}, u32[]{:S(2)}, u32[]{:S(2)}) collective-permute-start(bf16[128,512]{1,0:T(8,128)(2,1)S(1)} %get-tuple-element.164), channel_id=1, source_target_pairs={{6,0},{8,2},{10,4},{12,6},{14,8},{7,1},{9,3},{11,5},{13,7},{15,9},... | collective-permute-start | bytes 393224 | tf_op jit(solution)/shard_map/ppermute | solution.py:524
  181.0 44.0 %collective-permute-start.28 = (bf16[128,512]{1,0:T(8,128)(2,1)S(1)}, bf16[128,512]{1,0:T(8,128)(2,1)S(1)}, u32[]{:S(2)}, u32[]{:S(2)}) collective-permute-start(bf16[128,512]{1,0:T(8,128)(2,1)S(1)} %get-tuple-element.163), channel_id=1, source_target_pairs={{8,0},{10,2},{12,4},{14,6},{9,1},{11,3},{13,5},{15,7},{24,16},{26,... | collective-permute-start | bytes 393224 | tf_op jit(solution)/shard_map/ppermute | solution.py:524
  184.6 61.0 %collective-permute-start.40 = (bf16[2,48,1920]{2,1,0:T(8,128)(2,1)}, bf16[2,48,1920]{2,1,0:T(8,128)(2,1)}, u32[]{:S(2)}, u32[]{:S(2)}) collective-permute-start(bf16[2,48,1920]{2,1,0:T(8,128)(2,1)} %select_bitcast_fusion.11), channel_id=1, source_target_pairs={{0,4},{2,6},{4,0},{6,2},{8,12},{10,14},{12,8},{14,10},{1,5},{3,7},... | collective-permute-start | bytes 1105928 | tf_op jit(solution)/shard_map/ppermute | solution.py:40
  190.2 59.8 %collective-permute-start.43 = (bf16[2,48,1536]{2,1,0:T(8,128)(2,1)}, bf16[2,48,1536]{2,1,0:T(8,128)(2,1)}, u32[]{:S(2)}, u32[]{:S(2)}) collective-permute-start(bf16[2,48,1536]{2,1,0:T(8,128)(2,1)} %fusion.59), channel_id=1, source_target_pairs={{0,4},{2,6},{4,0},{6,2},{8,12},{10,14},{12,8},{14,10},{1,5},{3,7},... | collective-permute-start | bytes 884744 | tf_op jit(solution)/shard_map/ppermute | solution.py:40
  243.5 22.5 %collective-permute-start.30 = (bf16[8,48,384]{2,1,0:T(8,128)(2,1)S(1)}, bf16[8,48,384]{2,1,0:T(8,128)(2,1)S(1)}, u32[]{:S(2)}, u32[]{:S(2)}) collective-permute-start(bf16[8,48,384]{2,1,0:T(8,128)(2,1)S(1)} %select_bitcast_fusion.14), channel_id=1, source_target_pairs={{0,16},{16,0},{1,17},{17,1},{2,18},{18,2},{3,19},{19,3},{4,20},{20... | collective-permute-start | bytes 884744 | tf_op jit(solution)/shard_map/ppermute | solution.py:40
  245.6 37.1 %collective-permute-start.29 = (bf16[1024,768]{1,0:T(8,128)(2,1)}, bf16[1024,768]{1,0:T(8,128)(2,1)}, u32[]{:S(2)}, u32[]{:S(2)}) collective-permute-start(bf16[1024,768]{1,0:T(8,128)(2,1)} %get-tuple-element.143), channel_id=1, source_target_pairs={{0,1},{1,0},{2,3},{3,2},{4,5},{5,4},{6,7},{7,6},{8,9},{9,8},{10,11... | collective-permute-start | bytes 4718600 | tf_op jit(solution)/shard_map/ppermute | solution.py:40
  246.8 12.4 %collective-permute-start.41 = (bf16[1,48,1920]{2,1,0:T(8,128)(2,1)S(1)}, bf16[1,48,1920]{2,1,0:T(8,128)(2,1)S(1)}, u32[]{:S(2)}, u32[]{:S(2)}) collective-permute-start(bf16[1,48,1920]{2,1,0:T(8,128)(2,1)S(1)} %fusion.63), channel_id=1, source_target_pairs={{0,8},{2,10},{4,12},{6,14},{8,0},{10,2},{12,4},{14,6},{1,9},{3,11}... | collective-permute-start | bytes 552968 | tf_op jit(solution)/shard_map/ppermute | solution.py:40
  (67 other events, 535.2 us)
